TPU v7x, 32 devices: a whole 2x2x4 slice. The times are simulated.
32 devices in a mesh: groups: 2 (over x), lon: 16 (over z, y, core).
Axes of the slice: x: 2, y: 2, z: 4, core: 2. Of those that a mesh axis runs over, the one named last changes fastest.
Arguments:
- prior_state: bfloat16 [256, 226, 256], P(('groups', 'lon')), parts along dimension 0, may hold values from -6 to 6
- patch_embed: bfloat16 [2, 2, 226, 256], replicated, may hold values from -0.1875 to 0.1875
- conv_kernel: bfloat16 [2, 3, 3, 256], replicated, may hold values from -2 to 2
- conv_bias: bfloat16 [2, 256], replicated, may hold values from -2 to 2
- norm_gain: bfloat16 [2, 256], replicated, may hold values from 0.099609375 to 1.8984375
- mlp_up: bfloat16 [2, 256, 1024], replicated, may hold values from -0.375 to 0.375
- mlp_down: bfloat16 [2, 1024, 256], replicated, may hold values from -0.1875 to 0.1875
- patch_unembed: bfloat16 [256, 2, 2, 226], replicated, may hold values from -0.375 to 0.375
- emu_encode: bfloat16 [226, 1024], replicated, may hold values from -0.375 to 0.375
- chan_table: bfloat16 [22, 1024], replicated, may hold values from -5 to 5
- chan_head: bfloat16 [22, 1024], replicated, may hold values from -0.1875 to 0.1875
- head_bias: float32 [22], replicated, may hold values from -4 to 4
- obs_cells: int32 [131072], P(('groups', 'lon')), parts along dimension 0, may hold values from 0 to 2047
- obs_chans: int32 [131072], P(('groups', 'lon')), parts along dimension 0, may hold values from 0 to 21
- obs_values: float32 [131072], P(('groups', 'lon')), parts along dimension 0, may hold values from -6 to 6
- obs_counts: int32 [32], P(('groups', 'lon')), parts along dimension 0, may hold values from 1024 to 4096, as said below
Outputs:
- denoised: bfloat16 [256, 226, 256], P(('groups', 'lon')), parts along dimension 0
- state_gradient: float32 [256, 226, 256], P(('groups', 'lon')), parts along dimension 0
- innovations: float32 [131072], P(('groups', 'lon')), parts along dimension 0
There are 2 independent parts, one for each index of `groups`. A program takes and returns all parts, laid end to end along the dimension named above; an argument that names none is the same for every part. Nothing has to cross between parts.
Inputs may be any that keep to these rules, and one draw needn't show every extreme that they name: `obs_counts`: slots of a device at or beyond its count are unused; some device is full and some holds exactly a quarter.
All inputs are finite; a program needn't handle non-finite values.
Results may differ from a plain program's by a relative error of at most 0.017.
Values may be sent and summed in bfloat16 or wider, within the bound.
No kernel may reach another device: no remote copies, remote signals or barrier semaphores. Data moves between devices by JAX's collectives and lax.ppermute only.
A program may use at most 128 MiB of HBM per device.

v0:
```python
import jax
import jax.numpy as jnp
from jax import lax
from jax.sharding import PartitionSpec as P

LAYERS = 2


root_coef = 0.7978845608028654
cubic_coef = 0.044715
norm_eps = 1e-06


def extended(block, sides, width):
    for axis, dim in sides:
        count = lax.axis_size(axis)
        forward = [(i, i + 1) for i in range(count - 1)]
        forward.append((count - 1, 0))
        backward = [(target, source) for source, target in forward]
        low = lax.ppermute(
            lax.slice_in_dim(block, block.shape[dim] - width, None, axis=dim), axis, forward
        )
        high = lax.ppermute(lax.slice_in_dim(block, 0, width, axis=dim), axis, backward)
        block = jnp.concatenate([low, block, high], axis=dim)
    return block


def gelu_pair(pre_act):
    inner = root_coef * (pre_act + cubic_coef * pre_act * pre_act * pre_act)
    tangent = jnp.tanh(inner)
    value = 0.5 * pre_act * (1.0 + tangent)
    gelu_slope = 0.5 * (1.0 + tangent) + 0.5 * pre_act * (1.0 - tangent * tangent) * root_coef * (
        1.0 + 3.0 * cubic_coef * pre_act * pre_act
    )
    return (value, gelu_slope)


def lat_take(source, shift_by):
    if shift_by == 0:
        return source
    zero_col = jnp.zeros_like(source[..., :1])
    if shift_by < 0:
        return jnp.concatenate([zero_col, source[..., :-1]], axis=-1)
    return jnp.concatenate([source[..., 1:], zero_col], axis=-1)


def depthwise(padded, kernel, patch_rows):
    summed = jnp.zeros((patch_rows,) + padded.shape[1:], jnp.float32)
    for row_tap in range(3):
        rows_in = padded[row_tap : row_tap + patch_rows]
        for col_tap in range(3):
            summed = summed + kernel[row_tap, col_tap][None, :, None] * lat_take(
                rows_in, col_tap - 1
            )
    return summed


def embed_patches(prior_state, patch_embed):
    lon_rows, channels, lat_rows = prior_state.shape
    blocks = prior_state.reshape(lon_rows // 2, 2, channels, lat_rows // 2, 2)
    return jnp.einsum("iacjb,abce->iej", blocks, patch_embed, preferred_element_type=jnp.float32)


def unembed_patches(hidden, patch_unembed):
    pieces = jnp.einsum(
        "iej,eabc->iacjb", hidden, patch_unembed, preferred_element_type=jnp.float32
    )
    return pieces.reshape(pieces.shape[0] * 2, pieces.shape[2], pieces.shape[3] * 2)


def unembed_back(grad_round, patch_unembed):
    lon_rows, channels, lat_rows = grad_round.shape
    blocks = grad_round.reshape(lon_rows // 2, 2, channels, lat_rows // 2, 2)
    return jnp.einsum("iacjb,eabc->iej", blocks, patch_unembed, preferred_element_type=jnp.float32)


def embed_back(bottom_round, patch_embed):
    pieces = jnp.einsum(
        "iej,abce->iacjb", bottom_round, patch_embed, preferred_element_type=jnp.float32
    )
    return pieces.reshape(pieces.shape[0] * 2, pieces.shape[2], pieces.shape[3] * 2)


def layer_forward(padded, kernel, conv_bias, norm_gain, mlp_up, mlp_down, patch_rows):
    conv_out = (
        depthwise(padded.astype(jnp.float32), kernel.astype(jnp.float32), patch_rows)
        + conv_bias.astype(jnp.float32)[None, :, None]
    )
    inv_rms = lax.rsqrt(jnp.mean(conv_out * conv_out, axis=1, keepdims=True) + norm_eps)
    normed = (conv_out * inv_rms * norm_gain.astype(jnp.float32)[None, :, None]).astype(
        jnp.bfloat16
    )
    pre_act = jnp.einsum("iej,ef->ifj", normed, mlp_up, preferred_element_type=jnp.float32)
    activation, gelu_slope = gelu_pair(pre_act)
    output = conv_out + jnp.einsum(
        "ifj,fe->iej", activation.astype(jnp.bfloat16), mlp_down, preferred_element_type=jnp.float32
    )
    return (output.astype(jnp.bfloat16), conv_out, inv_rms, gelu_slope)


def layer_backward(upstream, conv_out, inv_rms, gelu_slope, norm_gain, mlp_up, mlp_down):
    act_grad = jnp.einsum(
        "iej,fe->ifj", upstream.astype(jnp.bfloat16), mlp_down, preferred_element_type=jnp.float32
    )
    pre_grad = (act_grad * gelu_slope).astype(jnp.bfloat16)
    norm_grad = jnp.einsum("ifj,ef->iej", pre_grad, mlp_up, preferred_element_type=jnp.float32)
    unit_norm = conv_out * inv_rms
    scaled_grad = norm_grad * norm_gain.astype(jnp.float32)[None, :, None]
    return upstream + inv_rms * (
        scaled_grad - unit_norm * jnp.mean(scaled_grad * unit_norm, axis=1, keepdims=True)
    )


def radiance_obs(
    columns, obs_chans, obs_values, live_mask, emu_encode, chan_table, chan_head, head_bias
):
    one_hot = (
        obs_chans[:, None] == jnp.arange(chan_table.shape[0], dtype=jnp.int32)[None, :]
    ).astype(jnp.bfloat16)
    pre_act = jnp.dot(columns, emu_encode, preferred_element_type=jnp.float32) + jnp.dot(
        one_hot, chan_table, preferred_element_type=jnp.float32
    )
    head_rows = jnp.dot(one_hot, chan_head, preferred_element_type=jnp.float32)
    head_offset = jnp.sum(one_hot.astype(jnp.float32) * head_bias[None, :], axis=1)
    activation, gelu_slope = gelu_pair(pre_act)
    predicted = jnp.sum(activation * head_rows, axis=1) + head_offset
    innovation = live_mask * (predicted - obs_values)
    pre_grad = (innovation[:, None] * head_rows * gelu_slope).astype(jnp.bfloat16)
    col_grad = lax.dot_general(
        pre_grad, emu_encode, (((1,), (1,)), ((), ())), preferred_element_type=jnp.float32
    ).astype(jnp.bfloat16)
    return (innovation, col_grad)


def radiance_blocks(columns, obs_chans, obs_values, live_mask, weights):
    slot_count = columns.shape[0]
    block_rows = min(slot_count, 1024)
    block_count = slot_count // block_rows

    def run_block(batch_items):
        return radiance_obs(
            batch_items[0],
            batch_items[1],
            batch_items[2],
            batch_items[3],
            weights[0],
            weights[1],
            weights[2],
            weights[3],
        )

    innovation, col_grad = lax.map(
        run_block,
        (
            columns.reshape(block_count, block_rows, -1),
            obs_chans.reshape(block_count, block_rows),
            obs_values.reshape(block_count, block_rows),
            live_mask.reshape(block_count, block_rows),
        ),
    )
    return (innovation.reshape(slot_count), col_grad.reshape(slot_count, -1))


def shards(
    prior_state,
    patch_embed,
    conv_kernel,
    conv_bias,
    norm_gain,
    mlp_up,
    mlp_down,
    patch_unembed,
    emu_encode,
    chan_table,
    chan_head,
    head_bias,
    obs_cells,
    obs_chans,
    obs_values,
    obs_counts,
):
    lon_size = lax.axis_size("lon")
    lon_rows, channels, lat_rows = prior_state.shape
    slot_count = obs_cells.shape[0]
    per_peer = slot_count // lon_size
    weights = (emu_encode, chan_table, chan_head, head_bias)
    hidden = embed_patches(prior_state, patch_embed).astype(jnp.bfloat16)
    patch_rows = hidden.shape[0]
    stored = []
    for depth in range(LAYERS):
        padded = extended(hidden, (("lon", 0),), 1)
        hidden, conv_out, inv_rms, gelu_slope = layer_forward(
            padded,
            conv_kernel[depth],
            conv_bias[depth],
            norm_gain[depth],
            mlp_up[depth],
            mlp_down[depth],
            patch_rows,
        )
        stored.append((conv_out, inv_rms, gelu_slope))
    denoised = (prior_state.astype(jnp.float32) + unembed_patches(hidden, patch_unembed)).astype(
        jnp.bfloat16
    )
    col_table = jnp.transpose(denoised, (0, 2, 1)).reshape(lon_rows * lat_rows, channels)
    live_mask = (jnp.arange(slot_count, dtype=jnp.int32) < obs_counts[0]).astype(jnp.float32)
    cells_in, chans_in = (
        lax.all_to_all(
            obs_cells.reshape(lon_size, per_peer), "lon", split_axis=0, concat_axis=0, tiled=True
        ),
        lax.all_to_all(
            obs_chans.reshape(lon_size, per_peer), "lon", split_axis=0, concat_axis=0, tiled=True
        ),
    )
    values_in, live_in = (
        lax.all_to_all(
            obs_values.reshape(lon_size, per_peer).astype(jnp.bfloat16),
            "lon",
            split_axis=0,
            concat_axis=0,
            tiled=True,
        ).astype(jnp.float32),
        lax.all_to_all(
            live_mask.reshape(lon_size, per_peer).astype(jnp.bfloat16),
            "lon",
            split_axis=0,
            concat_axis=0,
            tiled=True,
        ).astype(jnp.float32),
    )
    flat_cells = cells_in.reshape(slot_count)
    innovation_here, grads_here = radiance_blocks(
        col_table[flat_cells],
        chans_in.reshape(slot_count),
        values_in.reshape(slot_count),
        live_in.reshape(slot_count),
        weights,
    )
    innovations = lax.all_to_all(
        innovation_here.reshape(lon_size, per_peer), "lon", split_axis=0, concat_axis=0, tiled=True
    ).reshape(slot_count)
    grad_cells = (
        jnp.zeros((lon_rows * lat_rows, channels), jnp.float32)
        .at[flat_cells]
        .add(grads_here.astype(jnp.float32))
    )
    grad_hat = jnp.transpose(grad_cells.reshape(lon_rows, lat_rows, channels), (0, 2, 1))
    upstream = unembed_back(grad_hat.astype(jnp.bfloat16), patch_unembed)
    for depth in reversed(range(LAYERS)):
        conv_out, inv_rms, gelu_slope = stored[depth]
        conv_grad = layer_backward(
            upstream,
            conv_out,
            inv_rms,
            gelu_slope,
            norm_gain[depth],
            mlp_up[depth],
            mlp_down[depth],
        )
        padded = extended(conv_grad.astype(jnp.bfloat16), (("lon", 0),), 1).astype(conv_grad.dtype)
        upstream = depthwise(padded, conv_kernel[depth].astype(jnp.float32)[::-1, ::-1], patch_rows)
    state_gradient = grad_hat + embed_back(upstream.astype(jnp.bfloat16), patch_embed)
    return (denoised, state_gradient, innovations)


def solution(mesh):
    placed = (
        P(("groups", "lon"), None, None),
        P(),
        P(),
        P(),
        P(),
        P(),
        P(),
        P(),
        P(),
        P(),
        P(),
        P(),
        P(("groups", "lon")),
        P(("groups", "lon")),
        P(("groups", "lon")),
        P(("groups", "lon")),
    )
    return jax.shard_map(
        shards,
        mesh=mesh,
        in_specs=placed,
        out_specs=(
            P(("groups", "lon"), None, None),
            P(("groups", "lon"), None, None),
            P(("groups", "lon")),
        ),
        check_vma=False,
    )
```

profile of v0, /device:TPU:0, one launch (start us, length us, event | category | flops | bytes accessed | tf_op | source)
XLA Modules:
  0.0 239.5 jit_solution(2935321331939423879)
XLA Ops:
  3.5 5.5 %collective-permute-start.1 = (bf16[1,256,128]{2,1,0:T(8,128)(2,1)S(1)}, bf16[1,256,128]{2,1,0:T(8,128)(2,1)S(1)}, u32[]{:S(2)}, u32[]{:S(2)}) collective-permute-start(bf16[1,256,128]{2,1,0:T(8,128)(2,1)S(1)} %get-tuple-element.141), channel_id=1, source_target_pairs={{1,0},{2,1},{3,2},{4,3},{5,4},{6,5},{7,6},{8,7},{9,8},{10,9},{11,1... | collective-permute-start | bytes 196616 | tf_op jit(solution)/shard_map/ppermute | solution.py:23
  11.4 5.8 %all-to-all-start.1 = ((bf16[16,2,128]{2,1,0:T(2,128)(2,1)}), bf16[16,2,128]{2,1,0:T(2,128)(2,1)S(1)}, u32[]{:S(2)}, u32[]{:S(2)}) async-start(bf16[16,2,128]{2,1,0:T(2,128)(2,1)} %reshape.297), calls=%async_computation.1 | async-start | bytes 16384 | tf_op jit(solution)/shard_map/all_to_all | solution.py:223
  27.2 6.3 %all-to-all-done.3 = bf16[16,2,128]{2,1,0:T(2,128)(2,1)S(1)} async-done(((bf16[16,2,128]{2,1,0:T(2,128)(2,1)}), bf16[16,2,128]{2,1,0:T(2,128)(2,1)S(1)}, u32[]{:S(2)}, u32[]{:S(2)}) %all-to-all-start.3) | async-done | bytes 8224 | tf_op jit(solution)/shard_map/all_to_all | solution.py:216
  33.4 3.5 %all-to-all-start = ((s32[16,1,256]{2,1,0:T(1,128)}), s32[16,1,256]{2,1,0:T(1,128)S(1)}, u32[]{:S(2)}, u32[]{:S(2)}) async-start(s32[16,1,256]{2,1,0:T(1,128)} %bitcast.48), calls=%async_computation | async-start | bytes 32768 | tf_op jit(solution)/shard_map/all_to_all | solution.py:208
  37.0 6.4 %all-to-all-done = s32[16,1,256]{2,1,0:T(1,128)S(1)} async-done(((s32[16,1,256]{2,1,0:T(1,128)}), s32[16,1,256]{2,1,0:T(1,128)S(1)}, u32[]{:S(2)}, u32[]{:S(2)}) %all-to-all-start) | async-done | bytes 16416 | tf_op jit(solution)/shard_map/all_to_all | solution.py:208
  51.3 4.4 %collective-permute-start.3 = (bf16[1,256,128]{2,1,0:T(8,128)(2,1)S(1)}, bf16[1,256,128]{2,1,0:T(8,128)(2,1)S(1)}, u32[]{:S(2)}, u32[]{:S(2)}) collective-permute-start(bf16[1,256,128]{2,1,0:T(8,128)(2,1)S(1)} %get-tuple-element.139), channel_id=1, source_target_pairs={{1,0},{2,1},{3,2},{4,3},{5,4},{6,5},{7,6},{8,7},{9,8},{10,9},{11,1... | collective-permute-start | bytes 196616 | tf_op jit(solution)/shard_map/ppermute | solution.py:23
  57.6 4.5 %collective-permute-done.2 = bf16[1,256,128]{2,1,0:T(8,128)(2,1)S(1)} collective-permute-done((bf16[1,256,128]{2,1,0:T(8,128)(2,1)S(1)}, bf16[1,256,128]{2,1,0:T(8,128)(2,1)S(1)}, u32[]{:S(2)}, u32[]{:S(2)}) %collective-permute-start.2) | collective-permute-done | bytes 65568 | tf_op jit(solution)/shard_map/ppermute | solution.py:20
  65.7 4.3 %convolution_bitcast_fusion.1 = f32[4,2,226,128,2]{3,2,4,1,0:T(8,128)} fusion(f32[4,256,128]{2,1,0:T(8,128)S(1)} %get-tuple-element.103, f32[4,128,1024]{2,1,0:T(8,128)} %fusion.121, bf16[2,1024,256]{2,1,0:T(8,128)(2,1)} %param.24, bf16[256,2,2,226]{0,2,3,1:T(2,128)(2,1)S(1)} %copy-done.56), kind=kOutput, calls=%fused_computation.61 | convolution fusion | flops 510394368 | bytes 5459968 | tf_op jit(solution)/shard_map/iej,eabc->iacjb/dot_general | solution.py:65
  70.0 4.1 %copy.132 = f32[4,2,226,128,2]{2,4,3,1,0:T(2,128)} copy(f32[4,2,226,128,2]{3,2,4,1,0:T(8,128)} %convolution_bitcast_fusion.1) | data formatting | bytes 3702784 | tf_op jit(solution)/shard_map/iej,eabc->iacjb/transpose | solution.py:65
  74.1 3.7 %reshape.247 = f32[8,226,256]{1,2,0:T(8,128)} reshape(f32[4,2,226,128,2]{2,4,3,1,0:T(2,128)} %copy.132) | data formatting | bytes 3702784 | tf_op jit(solution)/shard_map/reshape | solution.py:68
  79.6 18.5 %gather_fusion = bf16[4096,226]{1,0:T(8,128)(2,1)} fusion(bf16[2048,226]{1,0:T(8,128)(2,1)S(1)} %bitcast.256, s32[4096]{0:T(1024)} %broadcast_clamp_fusion), kind=kCustom, calls=%fused_computation | custom fusion | bytes 3719168 | tf_op jit(solution)/shard_map/gather | solution.py:233
  98.1 55.0 %while.12 = (s32[]{:T(128)}, f32[4,1024]{1,0:T(4,128)}, bf16[4,1024,226]{1,2,0:T(8,128)(2,1)S(1)}, f32[4,1024]{1,0:T(4,128)S(1)}, bf16[4,1024,226]{2,1,0:T(8,128...) while((s32[]{:T(128)}, f32[4,1024]{1,0:T(4,128)}, ...), condition=%wide.region_5.6_spmd, body=%wide.region_2.5_spmd.sunk | while | flops 1073085440 | bytes 48443688 | solution.py:152
  106.3 5.6 %fusion.228 = bf16[4,1024,226]{1,2,0:T(8,128)(2,1)S(1)} fusion(bf16[4,1024,226]{1,2,0:T(8,128)(2,1)S(1)} %get-tuple-element.266, s32[]{:T(128)S(6)} %copy.193, bf16[226,1024]{1,0:T(8,128)(2,1)S(1)} %get-tuple-element.282, f32[1024,1024]{0,1:T(8,128)} %copy-done, f32[1024,1024]{0,1:T(8,128)} %get-tuple-element.249, f32[1024]{0:T(1024)S(1)} %get-tuple-element.250), kind=kOutput, calls=%fused_computation.16.clone.1 | convolution fusion | flops 495159296 | bytes 9342980 | tf_op jit(solution)/shard_map/while/body/eval_jaxpr/dot_general | solution.py:129
  120.0 5.6 %fusion.228 = bf16[4,1024,226]{1,2,0:T(8,128)(2,1)S(1)} fusion(bf16[4,1024,226]{1,2,0:T(8,128)(2,1)S(1)} %get-tuple-element.266, s32[]{:T(128)S(6)} %copy.193, bf16[226,1024]{1,0:T(8,128)(2,1)S(1)} %get-tuple-element.282, f32[1024,1024]{0,1:T(8,128)} %copy-done, f32[1024,1024]{0,1:T(8,128)} %get-tuple-element.249, f32[1024]{0:T(1024)S(1)} %get-tuple-element.250), kind=kOutput, calls=%fused_computation.16.clone.1 | convolution fusion | flops 495159296 | bytes 9342980 | tf_op jit(solution)/shard_map/while/body/eval_jaxpr/dot_general | solution.py:129
  133.8 5.6 %fusion.228 = bf16[4,1024,226]{1,2,0:T(8,128)(2,1)S(1)} fusion(bf16[4,1024,226]{1,2,0:T(8,128)(2,1)S(1)} %get-tuple-element.266, s32[]{:T(128)S(6)} %copy.193, bf16[226,1024]{1,0:T(8,128)(2,1)S(1)} %get-tuple-element.282, f32[1024,1024]{0,1:T(8,128)} %copy-done, f32[1024,1024]{0,1:T(8,128)} %get-tuple-element.249, f32[1024]{0:T(1024)S(1)} %get-tuple-element.250), kind=kOutput, calls=%fused_computation.16.clone.1 | convolution fusion | flops 495159296 | bytes 9342980 | tf_op jit(solution)/shard_map/while/body/eval_jaxpr/dot_general | solution.py:129
  147.5 5.6 %fusion.228 = bf16[4,1024,226]{1,2,0:T(8,128)(2,1)S(1)} fusion(bf16[4,1024,226]{1,2,0:T(8,128)(2,1)S(1)} %get-tuple-element.266, s32[]{:T(128)S(6)} %copy.193, bf16[226,1024]{1,0:T(8,128)(2,1)S(1)} %get-tuple-element.282, f32[1024,1024]{0,1:T(8,128)} %copy-done, f32[1024,1024]{0,1:T(8,128)} %get-tuple-element.249, f32[1024]{0:T(1024)S(1)} %get-tuple-element.250), kind=kOutput, calls=%fused_computation.16.clone.1 | convolution fusion | flops 495159296 | bytes 9342980 | tf_op jit(solution)/shard_map/while/body/eval_jaxpr/dot_general | solution.py:129
  156.1 23.3 %scatter_custom_fusion = f32[2048,226]{1,0:T(8,128)S(1)} fusion(s32[4096]{0:T(1024)S(1)} %bitcast.268, f32[4096,226]{1,0:T(8,128)} %bitcast.260, f32[]{:T(128)} %constant.30.clone.1), kind=kCustom, calls=%fused_computation.83 | custom fusion | flops 925696 | bytes 1851904 | tf_op jit(solution)/shard_map/scatter-add | solution.py:245
  185.6 4.7 %multiply_reduce_fusion.3 = (f32[4,128]{1,0:T(4,128)S(1)}, f32[4,256,128]{2,1,0:T(8,128)}) fusion(f32[4,256,128]{2,1,0:T(8,128)} %copy-done.3, f32[4,128]{1,0:T(4,128)S(1)} %add_rsqrt_fusion, f32[256]{0:T(256)S(1)} %bitcast.310, bf16[2,256,1024]{2,1,0:T(8,128)(2,1)} %param.23, f32[4,128,1024]{2,1,0:T(8,128)} %fusion.121, bf16[2,1024,256]{2,1,0:T(8,128)(2,1)} %param.24, ...), kind=kOutput, calls=%fused_computation.159 | convolution fusion | flops 547487232 | bytes 4723712 | tf_op jit(solution)/shard_map/ifj,ef->iej/dot_general | solution.py:106
  193.7 4.8 %collective-permute-done.4 = bf16[1,256,128]{2,1,0:T(8,128)(2,1)S(1)} collective-permute-done((bf16[1,256,128]{2,1,0:T(8,128)(2,1)S(1)}, bf16[1,256,128]{2,1,0:T(8,128)(2,1)S(1)}, u32[]{:S(2)}, u32[]{:S(2)}) %collective-permute-start.4) | collective-permute-done | bytes 65568 | tf_op jit(solution)/shard_map/ppermute | solution.py:20
  200.9 4.7 %multiply_reduce_fusion.2 = (f32[4,128]{1,0:T(4,128)S(1)}, f32[4,256,128]{2,1,0:T(8,128)}) fusion(f32[4,256,128]{2,1,0:T(8,128)} %copy-done.2, f32[4,128]{1,0:T(4,128)S(1)} %add_rsqrt_fusion.1, f32[256]{0:T(256)S(1)} %bitcast.308, bf16[2,256,1024]{2,1,0:T(8,128)(2,1)} %param.23, f32[4,128,1024]{2,1,0:T(8,128)} %copy-done.4, ...), kind=kOutput, calls=%fused_computation.157 | convolution fusion | flops 547487232 | bytes 4723712 | tf_op jit(solution)/shard_map/ifj,ef->iej/dot_general | solution.py:106
  209.5 5.3 %all-to-all-start.4 = ((f32[16,1,256]{2,1,0:T(1,128)}), f32[16,1,256]{2,1,0:T(1,128)S(1)}, u32[]{:S(2)}, u32[]{:S(2)}) async-start(f32[16,1,256]{2,1,0:T(1,128)} %all_to_all.32), calls=%async_computation.4 | async-start | bytes 32768 | tf_op jit(solution)/shard_map/all_to_all | solution.py:239
  216.3 5.1 %all-to-all-done.4 = f32[16,1,256]{2,1,0:T(1,128)S(1)} async-done(((f32[16,1,256]{2,1,0:T(1,128)}), f32[16,1,256]{2,1,0:T(1,128)S(1)}, u32[]{:S(2)}, u32[]{:S(2)}) %all-to-all-start.4) | async-done | bytes 16416 | tf_op jit(solution)/shard_map/all_to_all | solution.py:239
  225.0 4.1 %copy.145 = f32[4,2,226,128,2]{2,4,3,1,0:T(2,128)} copy(f32[4,2,226,128,2]{3,2,4,1,0:T(8,128)} %convolution_bitcast_fusion) | data formatting | bytes 3702784 | tf_op jit(solution)/shard_map/iej,abce->iacjb/transpose | solution.py:78
  229.1 3.7 %reshape.253 = f32[8,226,256]{1,2,0:T(8,128)} reshape(f32[4,2,226,128,2]{2,4,3,1,0:T(2,128)} %copy.145) | data formatting | bytes 3702784 | tf_op jit(solution)/shard_map/reshape | solution.py:81
  (244 shorter events, 92.2 us)
Async XLA Ops:
  3.5 43.5 %collective-permute-start.1 = (bf16[1,256,128]{2,1,0:T(8,128)(2,1)S(1)}, bf16[1,256,128]{2,1,0:T(8,128)(2,1)S(1)}, u32[]{:S(2)}, u32[]{:S(2)}) collective-permute-start(bf16[1,256,128]{2,1,0:T(8,128)(2,1)S(1)} %get-tuple-element.141), channel_id=1, source_target_pairs={{1,0},{2,1},{3,2},{4,3},{5,4},{6,5},{7,6},{8,7},{9,8},{10,9},{11,1... | collective-permute-start | bytes 196616 | tf_op jit(solution)/shard_map/ppermute | solution.py:23
  9.0 38.0 %collective-permute-start = (bf16[1,256,128]{2,1,0:T(8,128)(2,1)S(1)}, bf16[1,256,128]{2,1,0:T(8,128)(2,1)S(1)}, u32[]{:S(2)}, u32[]{:S(2)}) collective-permute-start(bf16[1,256,128]{2,1,0:T(8,128)(2,1)S(1)} %get-tuple-element.140), channel_id=1, source_target_pairs={{0,1},{1,2},{2,3},{3,4},{4,5},{5,6},{6,7},{7,8},{8,9},{9,10},{10,1... | collective-permute-start | bytes 196616 | tf_op jit(solution)/shard_map/ppermute | solution.py:20
  11.4 12.2 %all-to-all-start.1 = ((bf16[16,2,128]{2,1,0:T(2,128)(2,1)}), bf16[16,2,128]{2,1,0:T(2,128)(2,1)S(1)}, u32[]{:S(2)}, u32[]{:S(2)}) async-start(bf16[16,2,128]{2,1,0:T(2,128)(2,1)} %reshape.297), calls=%async_computation.1 | async-start | bytes 16384 | tf_op jit(solution)/shard_map/all_to_all | solution.py:223
  17.9 29.7 %copy-start.12 = (f32[1,1,256]{2,1,0:T(1,128)}, f32[1,1,256]{2,1,0:T(1,128)S(1)}, u32[]{:S(2)}) copy-start(f32[1,1,256]{2,1,0:T(1,128)S(1)} %get-tuple-element.151) | copy-start | bytes 3076
  17.9 29.7 %copy-start.14 = (f32[1,1,256]{2,1,0:T(1,128)}, f32[1,1,256]{2,1,0:T(1,128)S(1)}, u32[]{:S(2)}) copy-start(f32[1,1,256]{2,1,0:T(1,128)S(1)} %get-tuple-element.152) | copy-start | bytes 3076
  17.9 29.7 %copy-start.16 = (f32[1,1,256]{2,1,0:T(1,128)}, f32[1,1,256]{2,1,0:T(1,128)S(1)}, u32[]{:S(2)}) copy-start(f32[1,1,256]{2,1,0:T(1,128)S(1)} %get-tuple-element.153) | copy-start | bytes 3076
  17.9 29.7 %copy-start.18 = (f32[1,1,256]{2,1,0:T(1,128)}, f32[1,1,256]{2,1,0:T(1,128)S(1)}, u32[]{:S(2)}) copy-start(f32[1,1,256]{2,1,0:T(1,128)S(1)} %get-tuple-element.154) | copy-start | bytes 3076
  17.9 29.7 %copy-start.20 = (f32[1,1,256]{2,1,0:T(1,128)}, f32[1,1,256]{2,1,0:T(1,128)S(1)}, u32[]{:S(2)}) copy-start(f32[1,1,256]{2,1,0:T(1,128)S(1)} %get-tuple-element.155) | copy-start | bytes 3076
  17.9 29.7 %copy-start.22 = (f32[1,1,256]{2,1,0:T(1,128)}, f32[1,1,256]{2,1,0:T(1,128)S(1)}, u32[]{:S(2)}) copy-start(f32[1,1,256]{2,1,0:T(1,128)S(1)} %get-tuple-element.156) | copy-start | bytes 3076
  17.9 29.7 %copy-start.24 = (f32[1,1,256]{2,1,0:T(1,128)}, f32[1,1,256]{2,1,0:T(1,128)S(1)}, u32[]{:S(2)}) copy-start(f32[1,1,256]{2,1,0:T(1,128)S(1)} %get-tuple-element.157) | copy-start | bytes 3076
  17.9 29.7 %copy-start.26 = (f32[1,1,256]{2,1,0:T(1,128)}, f32[1,1,256]{2,1,0:T(1,128)S(1)}, u32[]{:S(2)}) copy-start(f32[1,1,256]{2,1,0:T(1,128)S(1)} %get-tuple-element.158) | copy-start | bytes 3076
  17.9 29.7 %copy-start.28 = (f32[1,1,256]{2,1,0:T(1,128)}, f32[1,1,256]{2,1,0:T(1,128)S(1)}, u32[]{:S(2)}) copy-start(f32[1,1,256]{2,1,0:T(1,128)S(1)} %get-tuple-element.159) | copy-start | bytes 3076
  18.6 44.1 %copy-start.30 = (f32[1,1,256]{2,1,0:T(1,128)}, f32[1,1,256]{2,1,0:T(1,128)S(1)}, u32[]{:S(2)}) copy-start(f32[1,1,256]{2,1,0:T(1,128)S(1)} %get-tuple-element.142) | copy-start | bytes 3076
  19.2 29.3 %copy-start.48 = (f32[1,256]{1,0:T(1,128)}, f32[1,256]{1,0:T(1,128)S(1)}, u32[]{:S(2)}) copy-start(f32[1,256]{1,0:T(1,128)S(1)} %get-tuple-element.163) | copy-start | bytes 3076
  23.6 9.8 %all-to-all-start.3 = ((bf16[16,2,128]{2,1,0:T(2,128)(2,1)}), bf16[16,2,128]{2,1,0:T(2,128)(2,1)S(1)}, u32[]{:S(2)}, u32[]{:S(2)}) async-start(bf16[16,2,128]{2,1,0:T(2,128)(2,1)} %reshape.299), calls=%async_computation.3 | async-start | bytes 16384 | tf_op jit(solution)/shard_map/all_to_all | solution.py:216
  33.4 10.0 %all-to-all-start = ((s32[16,1,256]{2,1,0:T(1,128)}), s32[16,1,256]{2,1,0:T(1,128)S(1)}, u32[]{:S(2)}, u32[]{:S(2)}) async-start(s32[16,1,256]{2,1,0:T(1,128)} %bitcast.48), calls=%async_computation | async-start | bytes 32768 | tf_op jit(solution)/shard_map/all_to_all | solution.py:208
  43.4 12.9 %all-to-all-start.2 = ((s32[16,1,256]{2,1,0:T(1,128)}), s32[16,1,256]{2,1,0:T(1,128)S(1)}, u32[]{:S(2)}, u32[]{:S(2)}) async-start(s32[16,1,256]{2,1,0:T(1,128)} %bitcast.55), calls=%async_computation.2 | async-start | bytes 32768 | tf_op jit(solution)/shard_map/all_to_all | solution.py:211
  51.3 6.3 %collective-permute-start.3 = (bf16[1,256,128]{2,1,0:T(8,128)(2,1)S(1)}, bf16[1,256,128]{2,1,0:T(8,128)(2,1)S(1)}, u32[]{:S(2)}, u32[]{:S(2)}) collective-permute-start(bf16[1,256,128]{2,1,0:T(8,128)(2,1)S(1)} %get-tuple-element.139), channel_id=1, source_target_pairs={{1,0},{2,1},{3,2},{4,3},{5,4},{6,5},{7,6},{8,7},{9,8},{10,9},{11,1... | collective-permute-start | bytes 196616 | tf_op jit(solution)/shard_map/ppermute | solution.py:23
  55.7 6.4 %collective-permute-start.2 = (bf16[1,256,128]{2,1,0:T(8,128)(2,1)S(1)}, bf16[1,256,128]{2,1,0:T(8,128)(2,1)S(1)}, u32[]{:S(2)}, u32[]{:S(2)}) collective-permute-start(bf16[1,256,128]{2,1,0:T(8,128)(2,1)S(1)} %get-tuple-element.138), channel_id=1, source_target_pairs={{0,1},{1,2},{2,3},{3,4},{4,5},{5,6},{6,7},{7,8},{8,9},{9,10},{10,1... | collective-permute-start | bytes 196616 | tf_op jit(solution)/shard_map/ppermute | solution.py:20
  191.7 2.0 collective-permute-start.5
  191.8 6.7 %collective-permute-start.4 = (bf16[1,256,128]{2,1,0:T(8,128)(2,1)S(1)}, bf16[1,256,128]{2,1,0:T(8,128)(2,1)S(1)}, u32[]{:S(2)}, u32[]{:S(2)}) collective-permute-start(bf16[1,256,128]{2,1,0:T(8,128)(2,1)S(1)} %get-tuple-element.136), channel_id=1, source_target_pairs={{0,1},{1,2},{2,3},{3,4},{4,5},{5,6},{6,7},{7,8},{8,9},{9,10},{10,1... | collective-permute-start | bytes 196616 | tf_op jit(solution)/shard_map/ppermute | solution.py:20
  207.6 13.7 %collective-permute-start.7 = (bf16[1,256,128]{2,1,0:T(8,128)(2,1)}, bf16[1,256,128]{2,1,0:T(8,128)(2,1)S(1)}, u32[]{:S(2)}, u32[]{:S(2)}) collective-permute-start(bf16[1,256,128]{2,1,0:T(8,128)(2,1)} %get-tuple-element.135), channel_id=1, source_target_pairs={{1,0},{2,1},{3,2},{4,3},{5,4},{6,5},{7,6},{8,7},{9,8},{10,9},{11,1... | collective-permute-start | bytes 196616 | tf_op jit(solution)/shard_map/ppermute | solution.py:23
  207.6 13.7 %collective-permute-start.6 = (bf16[1,256,128]{2,1,0:T(8,128)(2,1)}, bf16[1,256,128]{2,1,0:T(8,128)(2,1)S(1)}, u32[]{:S(2)}, u32[]{:S(2)}) collective-permute-start(bf16[1,256,128]{2,1,0:T(8,128)(2,1)} %get-tuple-element.134), channel_id=1, source_target_pairs={{0,1},{1,2},{2,3},{3,4},{4,5},{5,6},{6,7},{7,8},{8,9},{9,10},{10,1... | collective-permute-start | bytes 196616 | tf_op jit(solution)/shard_map/ppermute | solution.py:20
  209.5 11.8 %all-to-all-start.4 = ((f32[16,1,256]{2,1,0:T(1,128)}), f32[16,1,256]{2,1,0:T(1,128)S(1)}, u32[]{:S(2)}, u32[]{:S(2)}) async-start(f32[16,1,256]{2,1,0:T(1,128)} %all_to_all.32), calls=%async_computation.4 | async-start | bytes 32768 | tf_op jit(solution)/shard_map/all_to_all | solution.py:239
  (53 other events, 182.3 us)
where the time goes:
time: 242 us; the launch traced here: 239 us
  matrix products  68.6 us (28%)
  local copies, waits for them, and re-layouts  60.8 us (25%)
  other arithmetic  42.2 us (17%)
  waiting for transfers between devices  32.7 us (14%)
  starting transfers between devices  32.6 us (13%)
    scatter-add x1, other arithmetic, shards(): grad_cells = jnp.zeros((lon_rows * lat_rows, channels), jnp.float32).at[f...  23.3 us
    dot_general x4, matrix products, radiance_obs(): lax.dot_general(pre_grad, emu_encode, (((1,), (1,)), ((), ())), preferred...  22.3 us
    gather x1, local copies, waits for them, and re-layouts, shards(): col_table[flat_cells]  18.5 us
    dot_general x4, matrix products, radiance_obs(): head_rows = jnp.dot(one_hot, chan_head, preferred_element_type=jnp.float32)  13.4 us
    unnamed x121, local copies, waits for them, and re-layouts  9.99 us
    ppermute x4, starting transfers between devices, extended(): lax.ppermute(lax.slice_in_dim(block, 0, width, axis=dim), axis, backward)  9.96 us
    dot_general x2, matrix products, layer_backward(): jnp.einsum('ifj,ef->iej', pre_grad, mlp_up, preferred_element_type=jnp.fl...  9.32 us
    ppermute x4, waiting for transfers between devices, extended(): lax.ppermute(lax.slice_in_dim(block, block.shape[dim] - width, None, axis...  9.24 us
  transfers between devices with their start and end apart: 13, of which 8 were waited for; matrix products, arithmetic and copies ran while one was open for 4% of the time, Pallas kernels for 0%

commit v1 on v0

v1 whole, which is shorter than its diff:
```python
import functools

import jax
import jax.numpy as jnp
from jax import lax
from jax.experimental import pallas as pl
from jax.experimental.pallas import tpu as pltpu
from jax.sharding import PartitionSpec as P

LAYERS = 2
HALO = 2

root_coef = 0.7978845608028654
cubic_coef = 0.044715
norm_eps = 1e-06

F32 = jnp.float32
BF16 = jnp.bfloat16
GELU = jnp.bfloat16


def mm(a, b):
    return lax.dot_general(a, b, (((1,), (0,)), ((), ())), preferred_element_type=F32)


def mm_t(a, b):
    return lax.dot_general(a, b, (((1,), (1,)), ((), ())), preferred_element_type=F32)


def gelu_pair(pre):
    v = pre.astype(GELU)
    one = jnp.asarray(1.0, GELU)
    half = jnp.asarray(0.5, GELU)
    sq = v * v
    inner = v * (jnp.asarray(root_coef, GELU) + jnp.asarray(root_coef * cubic_coef, GELU) * sq)
    upper = half + half * jnp.tanh(inner)
    value = v * upper
    poly = jnp.asarray(2 * root_coef, GELU) + jnp.asarray(6 * root_coef * cubic_coef, GELU) * sq
    slope = upper + value * (one - upper) * poly
    return value, slope


def lat_split(size, dtype=BF16):
    row = lax.broadcasted_iota(jnp.int32, (size, size), 0)
    col = lax.broadcasted_iota(jnp.int32, (size, size), 1)
    half = size // 2
    want = jnp.where(row < half, 2 * row, 2 * (row - half) + 1)
    return jnp.where(col == want, 1.0, 0.0).astype(dtype)


def shift_rows(x, by):
    rows = x.shape[0]
    at = lax.broadcasted_iota(jnp.int32, x.shape, 0)
    if by == 1:
        return jnp.where(at == 0, 0.0, pltpu.roll(x, 1, 0))
    return jnp.where(at == rows - 1, 0.0, pltpu.roll(x, rows - 1, 0))


def conv_row(rows, taps):
    sums = []
    for q in range(3):
        total = taps[0][q] * rows[0]
        for p in (1, 2):
            total = total + taps[p][q] * rows[p]
        sums.append(total)
    return sums[1] + shift_rows(sums[0], 1) + shift_rows(sums[2], -1)


def load_taps(k_ref, layer, flip):
    def one(p, q):
        if flip:
            p, q = 2 - p, 2 - q
        return k_ref[p, q, :, :].astype(F32)[layer : layer + 1]

    return [[one(p, q) for q in range(3)] for p in range(3)]


def row_mean(x):
    width = x.shape[-1]
    return mm(x.astype(BF16), jnp.full((width, width), 1.0 / width, BF16))


def fill_lanes(xf, x_ref):
    chans, lon_rows, lat = x_ref.shape
    for k in range(lat // 128):
        part = x_ref[:, :, k * 128 : (k + 1) * 128].astype(F32)
        xf[k, 0 : chans * lon_rows, :] = part.reshape(chans * lon_rows, 128)
        xf[k, chans * lon_rows :, :] = jnp.zeros((xf.shape[1] - chans * lon_rows, 128), F32)


def lon_row(xf, lon, lon_rows):
    count = xf.shape[1] // lon_rows
    parts = [xf[k, pl.ds(lon, count, stride=lon_rows), :] for k in range(xf.shape[0])]
    return jnp.concatenate(parts, axis=1)


def put_lon_row(xf, lon, lon_rows, value):
    for k in range(xf.shape[0]):
        xf[k, pl.ds(lon, value.shape[0], stride=lon_rows), :] = value[:, k * 128 : (k + 1) * 128]


def embed_kernel(x_ref, w_ref, h_ref, first_ref, last_ref, xf, tcat):
    chans, lon_rows, lat = x_ref.shape
    padded = w_ref.shape[2]
    half = lat // 2
    fill_lanes(xf, x_ref)
    split = lat_split(lat)
    for lon in range(lon_rows):
        i, a = lon // 2, lon % 2
        tokens = mm_t(split, lon_row(xf, lon, lon_rows).astype(BF16)).astype(BF16)
        for b in range(2):
            tcat[i * half : (i + 1) * half, (2 * a + b) * padded : (2 * a + b + 1) * padded] = tokens[
                b * half : (b + 1) * half
            ]
    width = w_ref.shape[3]
    hidden = mm(tcat[...], w_ref[...].reshape(4 * padded, width)).astype(BF16)
    h_ref[...] = hidden
    first_ref[...] = hidden[: HALO * half]
    last_ref[...] = hidden[hidden.shape[0] - HALO * half :]


def split_kernel(x_ref, xp_ref, xf):
    chans, lon_rows, lat = x_ref.shape
    padded = xp_ref.shape[0]
    patch_rows = lon_rows // 2
    half = lat // 2
    fill_lanes(xf, x_ref)
    split = lat_split(lat)
    for lon in range(lon_rows):
        i, a = lon // 2, lon % 2
        part = mm_t(lon_row(xf, lon, lon_rows).astype(BF16), split).astype(BF16)
        for b in range(2):
            at = ((2 * a + b) * patch_rows + i) * half
            xp_ref[:, at : at + half] = part[:, b * half : (b + 1) * half]


def mlp_forward(layer, norm, conv, slope, up_ref, down_ref, store, tokens, block):
    for start in range(0, tokens, block):
        rows = pl.ds(start, block)
        value, tilt = gelu_pair(mm(norm[rows, :], up_ref[layer]))
        slope[rows, :] = tilt.astype(BF16)
        out = conv[rows, :] + mm(value.astype(BF16), down_ref[layer])
        store(start, out.astype(BF16))


def conv_norm_rows(count, source, layer, k_ref, bias_ref, gain_ref, conv, unit, scale, norm, half):
    taps = load_taps(k_ref, layer, False)
    bias = bias_ref[...].astype(F32)[layer : layer + 1]
    gain = gain_ref[...].astype(F32)[layer : layer + 1]

    def row(i, carry):
        out = conv_row([source[i + p].astype(F32) for p in range(3)], taps) + bias
        inv = lax.rsqrt(row_mean(out * out) + norm_eps)
        at = pl.ds(pl.multiple_of(i * half, half), half)
        u = out * inv
        conv[at, :] = out
        unit[at, :] = u
        scale[at, :] = inv
        norm[at, :] = (u * gain).astype(BF16)
        return carry

    lax.fori_loop(0, count, row, 0)


def mlp_backward(layer, upstream, unit, scale, slope, gain_ref, up_ref, down_ref):
    gain = gain_ref[...].astype(F32)[layer : layer + 1]
    pre = (mm_t(upstream.astype(BF16), down_ref[layer]) * slope.astype(F32)).astype(BF16)
    scaled = mm_t(pre, up_ref[layer]) * gain
    return upstream + scale * (scaled - unit * row_mean(scaled * unit))


def middle_kernel(
    h_ref, lo_ref, hi_ref, xp_ref, u_ref, k_ref, bias_ref, gain_ref, up_ref, down_ref,
    enc_ref, enct_ref, head_ref, headt_ref, hbias_ref, pay_ref,
    den_ref, innov_ref, cg_ref, first_ref, last_ref, unit0_ref, scale0_ref, slope0_ref, gradt_ref,
    h0, h1, conv, unit1, scale1, slope1, norm, h2, table, oht, gt, xf, gcell,
):
    chans, lon_rows, lat = den_ref.shape
    half = lat // 2
    patch_rows = lon_rows // 2
    padded = u_ref.shape[2]
    width = u_ref.shape[3]
    tokens = patch_rows * half
    wide = (patch_rows + 2) * half
    h0[0:HALO] = lo_ref[...].reshape(HALO, half, width)
    h0[HALO : HALO + patch_rows] = h_ref[...].reshape(patch_rows, half, width)
    h0[HALO + patch_rows :] = hi_ref[...].reshape(HALO, half, width)
    conv_norm_rows(
        patch_rows + 2, h0, 0, k_ref, bias_ref, gain_ref, conv, unit0_ref, scale0_ref, norm, half
    )

    def to_h1(start, out):
        h1[start // half : (start + out.shape[0]) // half] = out.reshape(-1, half, width)

    mlp_forward(0, norm, conv, slope0_ref, up_ref, down_ref, to_h1, wide, 2 * half)
    conv_norm_rows(
        patch_rows, h1, 1, k_ref, bias_ref, gain_ref, conv, unit1, scale1, norm, half
    )

    def to_h2(start, out):
        h2[start : start + out.shape[0], :] = out

    mlp_forward(1, norm, conv, slope1, up_ref, down_ref, to_h2, tokens, 2 * half)
    for ab in range(4):
        cols = slice(ab * tokens, (ab + 1) * tokens)
        table[:, cols] = (
            xp_ref[:, cols].astype(F32) + mm_t(u_ref[ab // 2, ab % 2], h2[...])
        ).astype(BF16)
    split = lat_split(lat)
    for lon in range(lon_rows):
        i, a = lon // 2, lon % 2
        at = [((2 * a + b) * patch_rows + i) * half for b in range(2)]
        both = jnp.concatenate([table[:, s : s + half] for s in at], axis=1)
        put_lon_row(xf, lon, lon_rows, mm(both, split))
    for k in range(lat // 128):
        part = xf[k, 0 : chans * lon_rows, :].reshape(chans, lon_rows, 128)
        den_ref[:, :, k * 128 : (k + 1) * 128] = part.astype(BF16)

    blocks, _, block = pay_ref.shape
    cells = lon_rows * lat
    head_pad = head_ref.shape[0]
    tail = padded - head_pad
    bias_col = hbias_ref[...]

    def radiance(p, carry):
        lanes = pl.ds(pl.multiple_of(p * block, block), block)
        pay = pay_ref[p]
        cell = pay[0:1].astype(jnp.int32)
        high = (cell // half).astype(F32)
        low = cell % half
        at = lax.broadcasted_iota(jnp.int32, (half, block), 0)
        key = jnp.where(at == low, high, -1.0).astype(BF16)
        for hi in range(cells // half):
            oht[hi * half : (hi + 1) * half, lanes] = jnp.where(
                key == jnp.asarray(hi, BF16), jnp.asarray(1, BF16), jnp.asarray(0, BF16)
            )
        columns = mm(table[...], oht[:, lanes])
        chan = pay[1:2].astype(jnp.int32)
        one_hot = jnp.where(
            lax.broadcasted_iota(jnp.int32, (head_pad, block), 0) == chan + (chans - tail), 1.0, 0.0
        )
        inputs = jnp.concatenate([columns[:tail], columns[tail:] + one_hot], axis=0).astype(BF16)
        pick = one_hot.astype(BF16)
        value, slope = gelu_pair(mm(enct_ref[...], inputs))
        heads = mm(headt_ref[...], pick).astype(GELU)
        found = mm(head_ref[...], value.astype(BF16)) + bias_col
        predicted = jnp.sum(found * one_hot, axis=0, keepdims=True)
        innov = pay[3:4] * (predicted - pay[2:3])
        innov_ref[pl.ds(p, 1), :] = innov
        grad = mm(enc_ref[...], (heads * slope).astype(BF16))
        gt[:, lanes] = (grad * innov).astype(BF16)
        return carry

    lax.fori_loop(0, blocks, radiance, 0)

    cell_block = 256

    def scatter(r, carry):
        rows = pl.ds(pl.multiple_of(r * cell_block, cell_block), cell_block)
        gcell[rows, :] = mm_t(oht[rows, :], gt[...]).astype(BF16)
        return carry

    lax.fori_loop(0, cells // cell_block, scatter, 0)
    eye = jnp.where(
        lax.broadcasted_iota(jnp.int32, (padded, padded), 0)
        == lax.broadcasted_iota(jnp.int32, (padded, padded), 1),
        1.0,
        0.0,
    ).astype(BF16)
    gradt_ref[...] = mm_t(eye, gcell[...]).astype(BF16)
    upstream = mm(gcell[0:tokens, :], u_ref[0, 0])
    for ab in range(1, 4):
        upstream = upstream + mm(gcell[ab * tokens : (ab + 1) * tokens, :], u_ref[ab // 2, ab % 2])
    grad = mlp_backward(
        1, upstream, unit1[...], scale1[...], slope1[...], gain_ref, up_ref, down_ref
    ).astype(BF16)
    cg_ref[...] = grad
    first_ref[...] = grad[: HALO * half]
    last_ref[...] = grad[tokens - HALO * half :]


def last_kernel(
    cg_ref, lo_ref, hi_ref, unit0_ref, scale0_ref, slope0_ref, gradt_ref,
    w_ref, k_ref, gain_ref, up_ref, down_ref, out_ref, c1, up1, c0, bottom, full, xf,
):
    rows_out, lat = out_ref.shape
    half = lat // 2
    padded = w_ref.shape[2]
    width = w_ref.shape[3]
    tokens = cg_ref.shape[0]
    patch_rows = tokens // half
    lon_rows = 2 * patch_rows
    chans = rows_out // lon_rows
    c1[0:HALO] = lo_ref[...].reshape(HALO, half, width)
    c1[HALO : HALO + patch_rows] = cg_ref[...].reshape(patch_rows, half, width)
    c1[HALO + patch_rows :] = hi_ref[...].reshape(HALO, half, width)
    taps = load_taps(k_ref, 1, True)

    def row1(i, carry):
        at = pl.ds(pl.multiple_of(i * half, half), half)
        up1[at, :] = conv_row([c1[i + p].astype(F32) for p in range(3)], taps)
        return carry

    lax.fori_loop(0, patch_rows + 2, row1, 0)
    for start in range(0, (patch_rows + 2) * half, 2 * half):
        at = pl.ds(start, 2 * half)
        grad = mlp_backward(
            0, up1[at, :], unit0_ref[at, :], scale0_ref[at, :], slope0_ref[at, :],
            gain_ref, up_ref, down_ref,
        )
        c0[start // half : start // half + 2] = grad.astype(BF16).reshape(2, half, width)
    taps0 = load_taps(k_ref, 0, True)

    def row0(i, carry):
        at = pl.ds(pl.multiple_of(i * half, half), half)
        bottom[at, :] = conv_row([c0[i + p].astype(F32) for p in range(3)], taps0).astype(BF16)
        return carry

    lax.fori_loop(0, patch_rows, row0, 0)
    for ab in range(4):
        cols = slice(ab * tokens, (ab + 1) * tokens)
        full[:, cols] = (
            gradt_ref[:, cols].astype(F32) + mm_t(w_ref[ab // 2, ab % 2], bottom[...])
        ).astype(BF16)
    split = lat_split(lat)
    for lon in range(lon_rows):
        i, a = lon // 2, lon % 2
        at = [((2 * a + b) * patch_rows + i) * half for b in range(2)]
        both = jnp.concatenate([full[:, s : s + half] for s in at], axis=1)
        put_lon_row(xf, lon, lon_rows, mm(both, split))
    for k in range(lat // 128):
        out_ref[:, k * 128 : (k + 1) * 128] = xf[k, 0:rows_out, :]


def call(kernel, outs, scratch, flops, nbytes, args, name):
    return pl.pallas_call(
        kernel,
        out_shape=[jax.ShapeDtypeStruct(shape, dtype) for shape, dtype in outs],
        scratch_shapes=[pltpu.VMEM(shape, dtype) for shape, dtype in scratch],
        cost_estimate=pl.CostEstimate(flops=flops, bytes_accessed=nbytes, transcendentals=0),
        name=name,
    )(*args)


def round_up(value, to):
    return -(-value // to) * to


def shards(
    prior_state, patch_embed, conv_kernel, conv_bias, norm_gain, mlp_up, mlp_down, patch_unembed,
    emu_encode, chan_table, chan_head, head_bias, obs_cells, obs_chans, obs_values, obs_counts,
):
    lon_size = lax.axis_size("lon")
    lon_rows, chans, lat = prior_state.shape
    slots = obs_cells.shape[0]
    per_peer = slots // lon_size
    width = patch_embed.shape[3]
    hidden_size = mlp_up.shape[2]
    emu, = emu_encode.shape[1:]
    nchan = chan_table.shape[0]
    half, patch_rows = lat // 2, lon_rows // 2
    tokens, cells = half * patch_rows, lat * lon_rows
    wide = tokens + 2 * half
    head_pad = 32
    padded = round_up(chans + nchan, 128)

    tile_lon, tile_lat = obs_cells // lat, obs_cells % lat
    place = ((tile_lon % 2 * 2 + tile_lat % 2) * patch_rows + tile_lon // 2) * half + tile_lat // 2
    live = (jnp.arange(slots, dtype=jnp.int32) < obs_counts[0]).astype(F32)
    sent = jnp.stack(
        [
            part.astype(F32).reshape(lon_size, per_peer)
            for part in (place, obs_chans, obs_values, live)
        ],
        axis=1,
    )
    pay = lax.all_to_all(sent, "lon", split_axis=0, concat_axis=0, tiled=True)
    group = max(1, 256 // per_peer)
    pay = pay.reshape(lon_size // group, group, 4, per_peer)
    pay = jnp.transpose(pay, (0, 2, 1, 3)).reshape(lon_size // group, 4, group * per_peer)

    forward = [(i, (i + 1) % lon_size) for i in range(lon_size)]
    backward = [(target, source) for source, target in forward]
    state = jnp.transpose(prior_state, (1, 0, 2))
    pad_c = ((0, 0), (0, 0), (0, padded - chans), (0, 0))
    w = jnp.pad(patch_embed, pad_c)
    u = jnp.pad(jnp.transpose(patch_unembed, (1, 2, 3, 0)), pad_c)
    taps = jnp.transpose(conv_kernel, (1, 2, 0, 3))
    hidden, first, last = call(
        embed_kernel,
        [((tokens, width), BF16), ((HALO * half, width), BF16), ((HALO * half, width), BF16)],
        [((lat // 128, padded * lon_rows, 128), F32), ((tokens, 4 * padded), BF16)],
        2 * tokens * 8 * padded * width, 2 * (state.size + w.size), (state, w), "embed",
    )
    low = lax.ppermute(last, "lon", forward)
    high = lax.ppermute(first, "lon", backward)
    (xp,) = call(
        split_kernel,
        [((padded, cells), BF16)],
        [((lat // 128, padded * lon_rows, 128), F32)],
        2 * tokens * 4 * padded * lat, 4 * state.size, (state,), "split",
    )
    rest = padded - chans - nchan
    enc = jnp.concatenate([emu_encode, chan_table, jnp.zeros((rest, emu), BF16)], axis=0)
    tail = padded - head_pad
    shift = chans - tail
    head = jnp.pad(chan_head, ((shift, head_pad - shift - nchan), (0, 0)))
    hbias = jnp.pad(head_bias, (shift, head_pad - shift - nchan)).reshape(head_pad, 1)
    (
        denoised, innov, grad, first, last, unit0, scale0, slope0, grad_t,
    ) = call(
        middle_kernel,
        [
            ((chans, lon_rows, lat), BF16),
            ((lon_size // group, group * per_peer), F32),
            ((tokens, width), BF16),
            ((HALO * half, width), BF16),
            ((HALO * half, width), BF16),
            ((wide, width), F32),
            ((wide, width), F32),
            ((wide, hidden_size), BF16),
            ((padded, cells), BF16),
        ],
        [
            ((patch_rows + 2 * HALO, half, width), BF16),
            ((patch_rows + 2, half, width), BF16),
            ((wide, width), F32),
            ((tokens, width), F32),
            ((tokens, width), F32),
            ((tokens, hidden_size), BF16),
            ((wide, width), BF16),
            ((tokens, width), BF16),
            ((padded, cells), BF16),
            ((cells, slots), BF16),
            ((padded, slots), BF16),
            ((lat // 128, padded * lon_rows, 128), F32),
            ((cells, padded), BF16),
        ],
        15 * 10**9, 10**7,
        (
            hidden, low, high, xp, u, taps, conv_bias, norm_gain, mlp_up, mlp_down,
            enc, enc.T, head, head.T, hbias, pay,
        ),
        "middle",
    )
    back = lax.ppermute(last, "lon", forward)
    ahead = lax.ppermute(first, "lon", backward)
    innovations = lax.all_to_all(
        innov.reshape(lon_size, per_peer), "lon", split_axis=0, concat_axis=0, tiled=True
    ).reshape(slots)
    (out,) = call(
        last_kernel,
        [((chans * lon_rows, lat), F32)],
        [
            ((patch_rows + 2 * HALO, half, width), BF16),
            ((wide, width), F32),
            ((patch_rows + 2, half, width), BF16),
            ((tokens, width), BF16),
            ((padded, cells), BF16),
            ((lat // 128, padded * lon_rows, 128), F32),
        ],
        4 * 10**9, 10**7,
        (grad, back, ahead, unit0, scale0, slope0, grad_t, w, taps, norm_gain, mlp_up, mlp_down),
        "last",
    )
    state_gradient = jnp.transpose(out.reshape(chans, lon_rows, lat), (1, 0, 2))
    return (jnp.transpose(denoised, (1, 0, 2)), state_gradient, innovations)


def solution(mesh):
    split = P(("groups", "lon"))
    placed = (split,) + (P(),) * 11 + (split,) * 4
    return jax.shard_map(
        shards, mesh=mesh, in_specs=placed, out_specs=(split,) * 3, check_vma=False
    )
```

time: 242 us -> 97.9 us (0.40)
  matrix products: 68.6 us -> 0 us
  Pallas kernels: 0 us -> 56.6 us
  local copies, waits for them, and re-layouts: 60.8 us -> 9.72 us
  other arithmetic: 42.2 us -> 4.13 us
  waiting for transfers between devices: 32.7 us -> 0.01 us
  starting transfers between devices: 32.6 us -> 16.3 us
  blocking collectives: 0 us -> 9.07 us
    dot_general x25 -> x0, matrix products: 68.6 us -> none  [the longest x4 22.3 us: radiance_obs(): lax.dot_general(pre_grad, emu_encode, (((1,), (1,)), ((), ())), preferred...]
    pallas_call x0 -> x4, Pallas kernels: none -> 56.6 us  [call(): pl.pallas_call(kernel, out_shape=[jax.ShapeDtypeStruct(shape, dtype) for...]
    scatter-add x1 -> x0, other arithmetic: 23.3 us -> none  [shards(): grad_cells = jnp.zeros((lon_rows * lat_rows, channels), jnp.float32).at[f...]
    all_to_all x5 -> x1, waiting for transfers between devices: 20.8 us -> 0.01 us  [shards(): pay = lax.all_to_all(sent, 'lon', split_axis=0, concat_axis=0, tiled=True)]
    gather x1 -> x0, local copies, waits for them, and re-layouts: 18.5 us -> none  [shards(): col_table[flat_cells]]
    all_to_all x5 -> x1, starting transfers between devices: 21.6 us -> 7.41 us  [shards(): pay = lax.all_to_all(sent, 'lon', split_axis=0, concat_axis=0, tiled=True)]
    ppermute x8 -> x4, waiting for transfers between devices: 11.9 us -> 0.01 us  [the longest x1 0.01 us: shards(): low = lax.ppermute(last, 'lon', forward)]
    reshape x4 -> x2, local copies, waits for them, and re-layouts: 10.3 us -> 0.76 us  [shards(): jnp.pad(head_bias, (shift, head_pad - shift - nchan)).reshape(head_pad, 1)]
  transfers between devices with their start and end apart: 13 -> 5, of which waited for: 8 -> 0; matrix products, arithmetic and copies ran while one was open for 4% -> 9% of each run, Pallas kernels for 0% -> 6%
where the time goes in v1:
time: 97.9 us; the launch traced here: 97.3 us
  Pallas kernels  56.6 us (58%)
  starting transfers between devices  16.3 us (17%)
  local copies, waits for them, and re-layouts  9.72 us (10%)
  blocking collectives  9.07 us (9%)
  other arithmetic  4.13 us (4%)
  between operations  1.43 us (1%)
    pallas_call x4, Pallas kernels, call(): pl.pallas_call(kernel, out_shape=[jax.ShapeDtypeStruct(shape, dtype) for...  56.6 us
    all_to_all x1, blocking collectives, shards(): lax.all_to_all(innov.reshape(lon_size, per_peer), 'lon', split_axis=0, co...  9.07 us
    all_to_all x1, starting transfers between devices, shards(): pay = lax.all_to_all(sent, 'lon', split_axis=0, concat_axis=0, tiled=True)  7.41 us
    ppermute x1, starting transfers between devices, shards(): ahead = lax.ppermute(first, 'lon', backward)  4.43 us
    ppermute x1, starting transfers between devices, shards(): high = lax.ppermute(first, 'lon', backward)  4.03 us
    unnamed x27, local copies, waits for them, and re-layouts  3.91 us
  transfers between devices with their start and end apart: 5, of which 0 were waited for; matrix products, arithmetic and copies ran while one was open for 9% of the time, Pallas kernels for 6%

profile of v1, /device:TPU:0, one launch (start us, length us, event | category | flops | bytes accessed | tf_op | source)
XLA Modules:
  0.0 97.3 jit_solution(4052844517152195164)
XLA Ops:
  1.3 0.8 fusion.6
  2.1 0.7 convert_element_type.24
  2.8 1.4 %pad_maximum_fusion = f32[16,4,256]{2,1,0:T(4,128)} fusion(f32[16,1,256]{2,1,0:T(1,128)S(1)} %compare_convert_fusion, f32[16,1,256]{2,1,0:T(1,128)} %bitcast.29, f32[16,1,256]{2,1,0:T(1,128)S(1)} %bitcast.27, f32[16,1,256]{2,1,0:T(1,128)S(1)} %bitcast.26), kind=kLoop, calls=%fused_computation.2 | loop fusion | flops 49152 | bytes 131072 | tf_op jit(solution)/shard_map/stack | solution.py:370
  4.2 7.4 %all-to-all-start = ((f32[16,4,256]{2,1,0:T(4,128)}), f32[16,4,256]{2,1,0:T(4,128)S(1)}, u32[]{:S(2)}, u32[]{:S(2)}) async-start(f32[16,4,256]{2,1,0:T(4,128)} %pad_maximum_fusion), calls=%async_computation | async-start | bytes 131072 | tf_op jit(solution)/shard_map/all_to_all | solution.py:377
  11.6 1.1 %copy.36 = bf16[2,2,226,256]{3,2,1,0:T(8,128)(2,1)S(1)} copy(bf16[2,2,226,256]{3,1,2,0:T(2,128)(2,1)} %param.17) | data formatting | bytes 925696 | tf_op args[1]
  12.8 0.8 pad.15.w_ref
  13.6 3.0 %embed.1 = (bf16[512,256]{1,0:T(8,128)(2,1)}, bf16[256,256]{1,0:T(8,128)(2,1)}, bf16[256,256]{1,0:T(8,128)(2,1)}) custom-call(bf16[226,8,256]{2,1,0:T(8,128)(2,1)} %bitcast.23, bf16[2,2,256,256]{3,2,1,0:T(8,128)(2,1)} %pad.15.w_ref), custom_call_target="tpu_custom_call" | custom-call | flops 536870912 | bytes 1449984 | tf_op jit(solution)/shard_map/embed/pallas_call | solution.py:336
  16.6 0.4 collective-permute-start
  17.0 4.0 %collective-permute-start.1 = (bf16[256,256]{1,0:T(8,128)(2,1)}, bf16[256,256]{1,0:T(8,128)(2,1)S(1)}, u32[]{:S(2)}, u32[]{:S(2)}) collective-permute-start(bf16[256,256]{1,0:T(8,128)(2,1)} %get-tuple-element.17), channel_id=1, source_target_pairs={{1,0},{2,1},{3,2},{4,3},{5,4},{6,5},{7,6},{8,7},{9,8},{10,9},{11,1... | collective-permute-start | bytes 393224 | tf_op jit(solution)/shard_map/ppermute | solution.py:396
  21.6 1.0 %fusion.17.enct_ref = bf16[1024,256]{1,0:T(8,128)(2,1)} fusion(bf16[256]{0:T(256)(128)(2,1)S(1)} %pad.25.clone, bf16[22,1024]{0,1:T(8,128)(2,1)S(1)} %copy.39, bf16[226,1024]{0,1:T(8,128)(2,1)S(1)} %copy.38), kind=kLoop, calls=%fused_computation.41 | loop fusion | flops 1572864 | bytes 1032704 | tf_op jit(solution)/shard_map/transpose | solution.py:442
  22.9 2.8 %split.1.xp_ref = bf16[256,2048]{1,0:T(8,128)(2,1)} custom-call(bf16[226,8,256]{2,1,0:T(8,128)(2,1)} %bitcast.24), custom_call_target="tpu_custom_call" | custom-call | flops 268435456 | bytes 1851392 | tf_op jit(solution)/shard_map/split/pallas_call | solution.py:336
  25.6 0.7 copy.44.hbias_ref
  26.7 0.7 pad.17.clone.head_ref
  27.4 0.8 pad.16.u_ref
  28.2 1.0 %copy.42.enc_ref = bf16[256,1024]{1,0:T(8,128)(2,1)} copy(bf16[256,1024]{0,1:T(8,128)(2,1)S(1)} %maximum_maximum_fusion) | data formatting | bytes 1048576 | tf_op jit(solution)/shard_map/concatenate | solution.py:404
  29.3 0.9 pad_bitcast_fusion.1.headt_ref
  30.2 0.6 copy-done.2
  30.9 42.2 %middle.1 = (bf16[226,8,256]{2,1,0:T(8,128)(2,1)}, f32[16,256]{1,0:T(8,128)}, bf16[512,256]{1,0:T(8,128)(2,1)}, bf16[256,256]{1,0:T(8,128)(2,1)}, bf16[256,256]{...) custom-call(bf16[512,256]{1,0:T(8,128)(2,1)} %get-tuple-element.15.h, ...), custom_call_target="tpu_custom_call" | custom-call | flops 15000000512 | bytes 10000000 | tf_op jit(solution)/shard_map/middle/pallas_call | solution.py:336
  73.1 4.4 %collective-permute-start.3 = (bf16[256,256]{1,0:T(8,128)(2,1)}, bf16[256,256]{1,0:T(8,128)(2,1)S(1)}, u32[]{:S(2)}, u32[]{:S(2)}) collective-permute-start(bf16[256,256]{1,0:T(8,128)(2,1)} %get-tuple-element.21), channel_id=1, source_target_pairs={{1,0},{2,1},{3,2},{4,3},{5,4},{6,5},{7,6},{8,7},{9,8},{10,9},{11,1... | collective-permute-start | bytes 393224 | tf_op jit(solution)/shard_map/ppermute | solution.py:447
  77.5 0.7 copy.45
  78.3 9.1 %all_to_all.14 = f32[16,1,256]{2,1,0:T(1,128)S(1)} all-to-all(f32[16,1,256]{2,1,0:T(1,128)S(1)} %copy.45), channel_id=1, replica_groups=mesh['groups'=2,'lon'=16] {'lon'}, dimensions={0} | all-to-all | bytes 32768 | tf_op jit(solution)/shard_map/all_to_all | solution.py:448
  87.4 0.6 copy-done.7
  88.1 8.6 %last.1 = f32[1808,256]{1,0:T(8,128)} custom-call(bf16[512,256]{1,0:T(8,128)(2,1)} %get-tuple-element.19.cg_ref, bf16[256,256]{1,0:T(8,128)(2,1)} %copy-done.7, bf16[256,256]{1,0:T(8,128)(2,1)} %copy-done.8, f32[768,256]{1,0:T(8,128)} %get-tuple-element.22.unit0_ref, f32[768,256]{1,0:T(8,128)} %get-tuple-element.23.scale0_ref, ...), custom_call_target="tpu_custom_call" | custom-call | flops 4000000000 | bytes 10000000 | tf_op jit(solution)/shard_map/last/pallas_call | solution.py:336
  96.7 0.6 copy.51
  (34 shorter events, 1.4 us)
Async XLA Ops:
  4.2 25.9 %all-to-all-start = ((f32[16,4,256]{2,1,0:T(4,128)}), f32[16,4,256]{2,1,0:T(4,128)S(1)}, u32[]{:S(2)}, u32[]{:S(2)}) async-start(f32[16,4,256]{2,1,0:T(4,128)} %pad_maximum_fusion), calls=%async_computation | async-start | bytes 131072 | tf_op jit(solution)/shard_map/all_to_all | solution.py:377
  11.6 9.4 %copy-start.3 = (bf16[22,1024]{1,0:T(8,128)(2,1)S(1)}, bf16[22,1024]{1,0:T(8,128)(2,1)}, u32[]{:S(2)}) copy-start(bf16[22,1024]{1,0:T(8,128)(2,1)} %param.25) | copy-start | bytes 135172
  12.7 8.5 %copy-start = (bf16[226,1024]{1,0:T(8,128)(2,1)S(1)}, bf16[226,1024]{1,0:T(8,128)(2,1)}, u32[]{:S(2)}) copy-start(bf16[226,1024]{1,0:T(8,128)(2,1)} %param.24) | copy-start | bytes 1388548
  16.6 13.6 %collective-permute-start = (bf16[256,256]{1,0:T(8,128)(2,1)}, bf16[256,256]{1,0:T(8,128)(2,1)S(1)}, u32[]{:S(2)}, u32[]{:S(2)}) collective-permute-start(bf16[256,256]{1,0:T(8,128)(2,1)} %get-tuple-element.16), channel_id=1, source_target_pairs={{0,1},{1,2},{2,3},{3,4},{4,5},{5,6},{6,7},{7,8},{8,9},{9,10},{10,1... | collective-permute-start | bytes 393224 | tf_op jit(solution)/shard_map/ppermute | solution.py:395
  17.0 13.2 %collective-permute-start.1 = (bf16[256,256]{1,0:T(8,128)(2,1)}, bf16[256,256]{1,0:T(8,128)(2,1)S(1)}, u32[]{:S(2)}, u32[]{:S(2)}) collective-permute-start(bf16[256,256]{1,0:T(8,128)(2,1)} %get-tuple-element.17), channel_id=1, source_target_pairs={{1,0},{2,1},{3,2},{4,3},{5,4},{6,5},{7,6},{8,7},{9,8},{10,9},{11,1... | collective-permute-start | bytes 393224 | tf_op jit(solution)/shard_map/ppermute | solution.py:396
  21.2 1.5 %copy-start.9 = (f32[22]{0:T(128)S(1)}, f32[22]{0:T(128)}, u32[]{:S(2)}) copy-start(f32[22]{0:T(128)} %param.27) | copy-start | bytes 268
  22.6 3.8 %copy-start.4 = (bf16[22,1024]{1,0:T(8,128)(2,1)S(1)}, bf16[22,1024]{1,0:T(8,128)(2,1)}, u32[]{:S(2)}) copy-start(bf16[22,1024]{1,0:T(8,128)(2,1)} %param.26) | copy-start | bytes 135172
  22.6 4.8 %copy-start.1 = (bf16[256,2,2,226]{0,2,3,1:T(2,128)(2,1)S(1)}, bf16[256,2,2,226]{0,2,3,1:T(2,128)(2,1)}, u32[]{:S(2)}) copy-start(bf16[256,2,2,226]{0,2,3,1:T(2,128)(2,1)} %param.23) | copy-start | bytes 1388548
  30.2 0.6 copy-start.2
  30.2 0.7 copy-start.5
  30.2 0.7 copy-start.6
  73.0 14.3 %collective-permute-start.2 = (bf16[256,256]{1,0:T(8,128)(2,1)}, bf16[256,256]{1,0:T(8,128)(2,1)S(1)}, u32[]{:S(2)}, u32[]{:S(2)}) collective-permute-start(bf16[256,256]{1,0:T(8,128)(2,1)} %get-tuple-element.20), channel_id=1, source_target_pairs={{0,1},{1,2},{2,3},{3,4},{4,5},{5,6},{6,7},{7,8},{8,9},{9,10},{10,1... | collective-permute-start | bytes 393224 | tf_op jit(solution)/shard_map/ppermute | solution.py:446
  73.1 14.2 %collective-permute-start.3 = (bf16[256,256]{1,0:T(8,128)(2,1)}, bf16[256,256]{1,0:T(8,128)(2,1)S(1)}, u32[]{:S(2)}, u32[]{:S(2)}) collective-permute-start(bf16[256,256]{1,0:T(8,128)(2,1)} %get-tuple-element.21), channel_id=1, source_target_pairs={{1,0},{2,1},{3,2},{4,3},{5,4},{6,5},{7,6},{8,7},{9,8},{10,9},{11,1... | collective-permute-start | bytes 393224 | tf_op jit(solution)/shard_map/ppermute | solution.py:447
  87.3 0.6 copy-start.7
  87.4 0.7 copy-start.8

commit v2 on v1

v2 whole, which is shorter than its diff:
```python
import functools

import jax
import jax.numpy as jnp
from jax import lax
from jax.experimental import pallas as pl
from jax.experimental.pallas import tpu as pltpu
from jax.sharding import PartitionSpec as P


HALO = 2

root_coef = 0.7978845608028654
cubic_coef = 0.044715
norm_eps = 1e-06

F32 = jnp.float32
BF16 = jnp.bfloat16
GELU = jnp.bfloat16


def mm(a, b):
    return lax.dot_general(a, b, (((1,), (0,)), ((), ())), preferred_element_type=F32)


def mm_t(a, b):
    return lax.dot_general(a, b, (((1,), (1,)), ((), ())), preferred_element_type=F32)


def gelu_pair(v):
    v = v.astype(GELU)
    one = jnp.asarray(1.0, GELU)
    sq = v * v
    cube = jnp.asarray(root_coef * cubic_coef, GELU) * sq
    inner = v * (jnp.asarray(root_coef, GELU) + cube)
    tangent = jnp.tanh(inner)
    upper = one + tangent
    poly = jnp.asarray(root_coef, GELU) + jnp.asarray(3 * root_coef * cubic_coef, GELU) * sq
    slope = upper * (one + v * poly * (one - tangent))
    return v * upper, slope


def copies(pairs, sems):
    started = [pltpu.make_async_copy(src, dst, sems.at[n]) for n, (src, dst) in enumerate(pairs)]
    for one in started:
        one.start()
    return started


def wide_dot(parts):
    return jnp.concatenate(parts, axis=1)


def lat_split(size, dtype=BF16):
    row = lax.broadcasted_iota(jnp.int32, (size, size), 0)
    col = lax.broadcasted_iota(jnp.int32, (size, size), 1)
    half = size // 2
    want = jnp.where(row < half, 2 * row, 2 * (row - half) + 1)
    return jnp.where(col == want, 1.0, 0.0).astype(dtype)


def shift_rows(x, by):
    rows = x.shape[0]
    at = lax.broadcasted_iota(jnp.int32, x.shape, 0)
    if by == 1:
        return jnp.where(at == 0, 0.0, pltpu.roll(x, 1, 0))
    return jnp.where(at == rows - 1, 0.0, pltpu.roll(x, rows - 1, 0))


def conv_row(rows, taps):
    sums = []
    for q in range(3):
        total = taps[0][q] * rows[0]
        for p in (1, 2):
            total = total + taps[p][q] * rows[p]
        sums.append(total)
    return sums[1] + shift_rows(sums[0], 1) + shift_rows(sums[2], -1)


def load_taps(k_ref, layer, flip):
    def one(p, q):
        if flip:
            p, q = 2 - p, 2 - q
        return k_ref[p, q, :, :].astype(F32)[layer : layer + 1]

    return [[one(p, q) for q in range(3)] for p in range(3)]


def whole(x, width):
    return jnp.concatenate([x] * (width // 128), axis=1)


def row_mean(x):
    width = x.shape[-1]
    return mm(x.astype(BF16), jnp.full((width, width), 1.0 / width, BF16))


def fill_lanes(xf, x, first, chans, lon_rows):
    for k in range(xf.shape[0]):
        part = x[first : first + chans, :, k * 128 : (k + 1) * 128].astype(F32)
        xf[k, first * lon_rows : (first + chans) * lon_rows, :] = part.reshape(chans * lon_rows, 128)


def lon_row(xf, lon, lon_rows):
    count = xf.shape[1] // lon_rows
    parts = [xf[k, pl.ds(lon, count, stride=lon_rows), :] for k in range(xf.shape[0])]
    return jnp.concatenate(parts, axis=1)


def put_lon_row(xf, lon, lon_rows, value):
    for k in range(xf.shape[0]):
        xf[k, pl.ds(lon, value.shape[0], stride=lon_rows), :] = value[:, k * 128 : (k + 1) * 128]


def fill_weights(out, w_ref, lanes):
    chans = w_ref.shape[1]
    for a in range(2):
        for k in range(out.shape[2] // 128):
            cols = slice(k * 128, (k + 1) * 128)
            lanes[k] = w_ref[a, :, :, cols].astype(F32).reshape(2 * chans, 128)
            for b in range(2):
                rows = lanes[k, pl.ds(b, chans, stride=2), :]
                out[2 * a + b, 0:chans, cols] = rows.astype(BF16)
    for ab in range(4):
        out[ab, chans:, :] = jnp.zeros((out.shape[1] - chans, out.shape[2]), BF16)


def embed_kernel(
    peers, *refs
):
    packed = peers is not None
    if packed:
        count_ref, cells_ref, chans_ref, values_ref, x_hbm, w_hbm = refs[:6]
        h_ref, first_ref, last_ref, pay_ref, xp_out, wp_out, *scratch = refs[6:]
    else:
        x_hbm, w_hbm, h_ref, first_ref, last_ref, xp_out, wp_out, *scratch = refs
    xf, tcat, wp, xp_ref, x_ref, w_ref, lanes, in_sems, sems = scratch
    chans, lon_rows, lat = x_ref.shape
    padded, width = wp.shape[1:]
    half = lat // 2
    edges = [chans * n // 4 for n in range(5)]
    spans = [pl.ds(lo, hi - lo) for lo, hi in zip(edges, edges[1:])]
    fetched = copies([(x_hbm.at[at], x_ref.at[at]) for at in spans] + [(w_hbm, w_ref)], in_sems)
    for k in range(lat // 128):
        xf[k, chans * lon_rows :, :] = jnp.zeros(((padded - chans) * lon_rows, 128), F32)
    for n in range(4):
        fetched[n].wait()
        fill_lanes(xf, x_ref, edges[n], edges[n + 1] - edges[n], lon_rows)
    split = lat_split(lat)
    for lon in range(lon_rows):
        i, a = lon // 2, lon % 2
        rows = lon_row(xf, lon, lon_rows).astype(BF16)
        tokens = mm_t(split, rows).astype(BF16)
        part = mm_t(rows, split).astype(BF16)
        for b in range(2):
            xp_ref[(2 * a + b) * (lon_rows // 2) + i] = part[:, b * half : (b + 1) * half]
            tcat[i * half : (i + 1) * half, (2 * a + b) * padded : (2 * a + b + 1) * padded] = tokens[
                b * half : (b + 1) * half
            ]
    fetched[4].wait()
    fill_weights(wp, w_ref, lanes)
    sent = copies([(xp_ref, xp_out), (wp, wp_out)], sems)
    hidden = mm(tcat[...], wp[...].reshape(4 * padded, width)).astype(BF16)
    h_ref[...] = hidden
    first_ref[...] = hidden[: HALO * half]
    last_ref[...] = hidden[hidden.shape[0] - HALO * half :]
    if not packed:
        for one in sent:
            one.wait()
        return
    rows, wide = cells_ref.shape
    per = rows // peers
    for part in range(per):
        at = pl.ds(part, peers, stride=per)
        cell = cells_ref[at, :]
        tile_lon, tile_lat = cell // lat, cell % lat
        place = (
            (tile_lon % 2 * 2 + tile_lat % 2) * (lon_rows // 2) + tile_lon // 2
        ) * half + tile_lat // 2
        slot = (
            lax.broadcasted_iota(jnp.int32, (peers, wide), 0) * (per * wide)
            + part * wide
            + lax.broadcasted_iota(jnp.int32, (peers, wide), 1)
        )
        live = jnp.where(slot < count_ref[0], 1.0, 0.0)
        kinds = (place.astype(F32), chans_ref[at, :].astype(F32), values_ref[at, :], live)
        for kind, value in enumerate(kinds):
            pay_ref[pl.ds(kind * per + part, peers, stride=4 * per), :] = value
    for one in sent:
        one.wait()


def mlp_forward(layer, norm, conv, slope, up_ref, down_ref, store, tokens, block):
    for start in range(0, tokens, block):
        rows = pl.ds(start, block)
        value, tilt = gelu_pair(mm(norm[rows, :], up_ref[layer]))
        slope[rows, :] = tilt.astype(BF16)
        out = conv[rows, :] + 0.5 * mm(value.astype(BF16), down_ref[layer])
        store(start, out.astype(BF16))


def conv_norm_rows(count, source, layer, k_ref, bias_ref, gain_ref, conv, unit, scale, norm, half):
    taps = load_taps(k_ref, layer, False)
    bias = bias_ref[...].astype(F32)[layer : layer + 1]
    gain = gain_ref[...].astype(F32)[layer : layer + 1]

    def row(i, carry):
        out = conv_row([source[i + p].astype(F32) for p in range(3)], taps) + bias
        inv = lax.rsqrt(row_mean(out * out) + norm_eps)
        at = pl.ds(pl.multiple_of(i * half, half), half)
        u = out * inv
        conv[at, :] = out
        unit[at, :] = u.astype(BF16)
        scale[at, :] = inv[:, 0:128]
        norm[at, :] = (u * gain).astype(BF16)
        return carry

    lax.fori_loop(0, count, row, 0)


def mlp_backward(upstream, unit, scale, slope, half_gain, up, down):
    pre = (mm_t(upstream.astype(BF16), down) * slope.astype(F32)).astype(BF16)
    scaled = mm_t(pre, up) * half_gain
    return upstream + scale * (scaled - unit * row_mean(scaled * unit))


def forward_kernel(
    h_ref, lo_ref, hi_ref, k_ref, bias_ref, gain_ref, xp_hbm, u_hbm, up_hbm, down_hbm,
    table_out, unit0_out, scale0_out, slope0_out, unit1_out, scale1_out, slope1_out, up_out,
    h0, h1, conv, norm, h2, up, xp_ref, u_ref, up_ref, down_ref,
    table_ref, unit0, scale0, slope0, unit1, scale1, slope1, lanes, sems, out_sems,
):
    fetched = copies(
        [(up_hbm, up_ref), (down_hbm, down_ref), (u_hbm, u_ref), (xp_hbm, xp_ref)], sems
    )
    _, _, half = table_ref.shape
    width = up.shape[2]
    tokens = h_ref.shape[0]
    patch_rows = tokens // half
    wide = (patch_rows + 2) * half
    h0[0:HALO] = lo_ref[...].reshape(HALO, half, width)
    h0[HALO : HALO + patch_rows] = h_ref[...].reshape(patch_rows, half, width)
    h0[HALO + patch_rows :] = hi_ref[...].reshape(HALO, half, width)
    conv_norm_rows(
        patch_rows + 2, h0, 0, k_ref, bias_ref, gain_ref, conv, unit0, scale0, norm, half
    )

    def to_h1(start, out):
        h1[start // half : (start + out.shape[0]) // half] = out.reshape(-1, half, width)

    fetched[0].wait()
    fetched[1].wait()
    mlp_forward(0, norm, conv, slope0, up_ref, down_ref, to_h1, wide, 2 * half)
    sent = copies(
        [(unit0, unit0_out), (scale0, scale0_out), (slope0, slope0_out)], out_sems.at[pl.ds(0, 3)]
    )
    fetched[2].wait()
    fill_weights(up, u_ref, lanes)
    sent += copies([(up, up_out)], out_sems.at[pl.ds(7, 1)])
    conv_norm_rows(
        patch_rows, h1, 1, k_ref, bias_ref, gain_ref, conv, unit1, scale1, norm, half
    )

    def to_h2(start, out):
        h2[start : start + out.shape[0], :] = out

    mlp_forward(1, norm, conv, slope1, up_ref, down_ref, to_h2, tokens, 2 * half)
    sent += copies(
        [(unit1, unit1_out), (scale1, scale1_out), (slope1, slope1_out)], out_sems.at[pl.ds(3, 3)]
    )
    fetched[3].wait()
    for ab in range(4):
        part = mm_t(up[ab], h2[...])
        for i in range(patch_rows):
            at = ab * patch_rows + i
            mine = part[:, i * half : (i + 1) * half]
            table_ref[at] = (xp_ref[at].astype(F32) + mine).astype(BF16)
    sent += copies([(table_ref, table_out)], out_sems.at[pl.ds(6, 1)])
    for one in sent:
        one.wait()


def is_cell(key, high):
    return jnp.where(key == jnp.asarray(high, BF16), jnp.asarray(1, BF16), jnp.asarray(0, BF16))


def identity(size):
    row = lax.broadcasted_iota(jnp.int32, (size, size), 0)
    col = lax.broadcasted_iota(jnp.int32, (size, size), 1)
    return jnp.where(row == col, 1.0, 0.0).astype(BF16)


def radiance_kernel(
    pay_ref, enc_ref, tab_ref, head_ref, hbias_ref, gain_ref,
    table_hbm, u_hbm, up_hbm, down_hbm, unit1_hbm, scale1_hbm, slope1_hbm,
    innov_ref, cg_ref, first_ref, last_ref, gradt_ref, den_out,
    enc, enct, heads, headst, keys, gt, gcell, up, xf, den, inputs, pre, out, value, slope,
    table_ref, up_ref, down_ref, unit1_ref, scale1_ref, slope1_ref, sems, out_sems,
):
    fetched = copies(
        [
            (table_hbm, table_ref),
            (u_hbm, up),
            (up_hbm.at[pl.ds(1, 1)], up_ref),
            (down_hbm.at[pl.ds(1, 1)], down_ref),
            (unit1_hbm, unit1_ref),
            (scale1_hbm, scale1_ref),
            (slope1_hbm, slope1_ref),
        ],
        sems,
    )
    chans, emu = enc_ref.shape
    nchan = tab_ref.shape[0]
    cell_blocks, padded, half = table_ref.shape
    blocks = pay_ref.shape[0]
    block = 2 * 128
    tokens, width = cg_ref.shape
    lon_rows, lat = den.shape[1:]
    patch_rows = lon_rows // 2
    one_at = round_up(chans, 8)
    tail = padded - heads.shape[1]
    shift = one_at - tail
    zeros = jnp.zeros((one_at - chans, 128), BF16)
    eye = identity(padded)
    for k in range(emu // 128):
        cols = slice(k * 128, (k + 1) * 128)
        enc[k, 0:chans, :] = enc_ref[:, cols]
        enc[k, chans:one_at, :] = zeros
        enc[k, one_at : one_at + nchan, :] = tab_ref[:, cols]
        enc[k, one_at + nchan :, :] = jnp.zeros((padded - one_at - nchan, 128), BF16)
        heads[k, 0:shift, :] = jnp.zeros((shift, 128), BF16)
        heads[k, shift : shift + nchan, :] = head_ref[:, cols]
        heads[k, shift + nchan :, :] = jnp.zeros((heads.shape[1] - shift - nchan, 128), BF16)
    for k in range(0, emu // 128, padded // 128):
        rows = slice(k * 128, k * 128 + padded)
        flip = mm_t(eye, wide_dot([enc[k + n] for n in range(padded // 128)])).astype(BF16)
        for n in range(padded // 128):
            enct[n, rows, :] = flip[:, n * 128 : (n + 1) * 128]
        headst[rows, :] = mm_t(eye, wide_dot([heads[k + n] for n in range(padded // 128)])).astype(BF16)
    rows = heads.shape[1]
    spot = lax.broadcasted_iota(jnp.int32, (rows, nchan), 0)
    lane = lax.broadcasted_iota(jnp.int32, (rows, nchan), 1)
    bias_row = jnp.broadcast_to(hbias_ref[...], (rows, nchan))
    bias_col = jnp.sum(jnp.where(spot == lane + shift, bias_row, 0.0), axis=1, keepdims=True)

    fetched[0].wait()
    split = lat_split(lat)
    for lon in range(lon_rows):
        i, a = lon // 2, lon % 2
        both = wide_dot([table_ref[(2 * a + b) * patch_rows + i] for b in range(2)])
        put_lon_row(xf, lon, lon_rows, mm(both, split))
    for k in range(lat // 128):
        part = xf[k, 0 : chans * lon_rows, :].reshape(chans, lon_rows, 128)
        den[:, :, k * 128 : (k + 1) * 128] = part.astype(BF16)
    sent = copies([(den, den_out)], out_sems)

    def row_of(pay, kind):
        return wide_dot([pay[2 * kind : 2 * kind + 1], pay[2 * kind + 1 : 2 * kind + 2]])

    def one_hot_of(pay):
        chan = row_of(pay, 1).astype(jnp.int32)
        at = lax.broadcasted_iota(jnp.int32, (rows, block), 0)
        return jnp.where(at == chan + shift, 1.0, 0.0)

    def gather(p):
        pay = pay_ref[p]
        cell = row_of(pay, 0).astype(jnp.int32)
        high = (cell // half).astype(F32)
        low = cell % half
        at = lax.broadcasted_iota(jnp.int32, (half, block), 0)
        key = jnp.where(at == low, high, -1.0).astype(BF16)
        for n in range(2):
            keys[2 * p + n] = key[:, n * 128 : (n + 1) * 128]
        picks = jnp.concatenate([is_cell(key, k) for k in range(cell_blocks)], axis=0)
        columns = mm(wide_dot([table_ref[k] for k in range(cell_blocks)]), picks)
        one_hot = one_hot_of(pay)
        inputs[0:tail, :] = columns[:tail].astype(BF16)
        inputs[tail:, :] = (columns[tail:] + one_hot).astype(BF16)

    def first_layer(p):
        one_hot = one_hot_of(pay_ref[p])
        pre[...] = mm(wide_dot([enct[n] for n in range(padded // 128)]), inputs[...]).astype(GELU)
        out[...] = mm(headst[:, 0:rows], one_hot.astype(BF16)).astype(GELU)

    def activate():
        for start in range(0, emu, 32):
            at = pl.ds(start, 32)
            act, tilt = gelu_pair(pre[at, :])
            value[at, :] = act.astype(BF16)
            slope[at, :] = (tilt * out[at, :]).astype(BF16)

    def finish(p):
        pay = pay_ref[p]
        found = mm(wide_dot([heads[k] for k in range(emu // 128)]), value[...])
        found = (0.5 * found + bias_col) * one_hot_of(pay)
        predicted = jnp.sum(found, axis=0, keepdims=True)
        innov = row_of(pay, 3) * (predicted - row_of(pay, 2))
        grad = mm(wide_dot([enc[k] for k in range(emu // 128)]), slope[...])
        grad = (grad * (0.5 * innov)).astype(BF16)
        for n in range(2):
            innov_ref[pl.ds(2 * p + n, 1), :] = innov[:, n * 128 : (n + 1) * 128]
            gt[2 * p + n] = grad[:, n * 128 : (n + 1) * 128]

    def steps(p, carry):
        finish(lax.rem(p + blocks - 3, blocks))
        activate()
        first_layer(jnp.clip(p - 1, 0, blocks - 1))
        gather(jnp.minimum(p, blocks - 1))
        return carry

    lax.fori_loop(0, blocks + 3, steps, 0)

    lane_blocks = keys.shape[0]

    def scatter(r, carry):
        key = wide_dot([keys[k] for k in range(lane_blocks)])
        high = (2 * r).astype(F32)
        picks = []
        for n in range(2):
            want = jnp.full((1, 1), high + n, F32).astype(BF16)
            picks.append(jnp.where(key == want, jnp.asarray(1, BF16), jnp.asarray(0, BF16)))
        lhs = jnp.concatenate(picks, axis=0)
        out = mm_t(lhs, wide_dot([gt[k] for k in range(lane_blocks)])).astype(BF16)
        at = pl.ds(pl.multiple_of(r * 2 * half, 2 * half), 2 * half)
        for n in range(padded // 128):
            gcell[n, at, :] = out[:, n * 128 : (n + 1) * 128]
        return carry

    lax.fori_loop(0, cell_blocks // 2, scatter, 0)
    for one in fetched[1:]:
        one.wait()
    flip = mm_t(eye, wide_dot([gcell[n] for n in range(padded // 128)])).astype(BF16)
    for k in range(cell_blocks):
        gradt_ref[k] = flip[:, k * half : (k + 1) * half]
    upstream = None
    for ab in range(4):
        at = slice(ab * tokens, (ab + 1) * tokens)
        part = mm(wide_dot([gcell[n, at, :] for n in range(padded // 128)]), up[ab])
        upstream = part if upstream is None else upstream + part
    grad = mlp_backward(
        upstream, unit1_ref[...].astype(F32), whole(scale1_ref[...], width), slope1_ref[...],
        0.5 * gain_ref[...].astype(F32)[1:2], up_ref[0], down_ref[0],
    ).astype(BF16)
    cg_ref[...] = grad
    first_ref[...] = grad[: HALO * half]
    last_ref[...] = grad[tokens - HALO * half :]
    sent[0].wait()


def last_kernel(
    cg_ref, lo_ref, hi_ref, k_ref, gain_ref,
    unit0_hbm, scale0_hbm, slope0_hbm, gradt_hbm, w_hbm, up_hbm, down_hbm, out_hbm,
    c1, up1, c0, bottom, full, xf, wp,
    unit0_ref, scale0_ref, slope0_ref, gradt_ref, up_ref, down_ref, sems, out_sems,
):
    wide, block = up1.shape[0], 2 * c1.shape[1]
    kept = [(slope0_hbm, slope0_ref), (unit0_hbm, unit0_ref), (scale0_hbm, scale0_ref)]
    pairs = [(down_hbm.at[pl.ds(0, 1)], down_ref), (up_hbm.at[pl.ds(0, 1)], up_ref)]
    for start in range(0, wide, block):
        pairs += [(src.at[pl.ds(start, block)], dst.at[pl.ds(start, block)]) for src, dst in kept]
    fetched = copies(pairs + [(w_hbm, wp), (gradt_hbm, gradt_ref)], sems)
    rows_out, lat = out_hbm.shape
    half = lat // 2
    _, width = wp.shape[1:]
    tokens = cg_ref.shape[0]
    patch_rows = tokens // half
    lon_rows = 2 * patch_rows
    c1[0:HALO] = lo_ref[...].reshape(HALO, half, width)
    c1[HALO : HALO + patch_rows] = cg_ref[...].reshape(patch_rows, half, width)
    c1[HALO + patch_rows :] = hi_ref[...].reshape(HALO, half, width)
    taps = load_taps(k_ref, 1, True)

    def row1(i, carry):
        at = pl.ds(pl.multiple_of(i * half, half), half)
        up1[at, :] = conv_row([c1[i + p].astype(F32) for p in range(3)], taps)
        return carry

    lax.fori_loop(0, patch_rows + 2, row1, 0)
    half_gain = 0.5 * gain_ref[...].astype(F32)[0:1]
    fetched[0].wait()
    fetched[1].wait()
    for start in range(0, wide, block):
        at = pl.ds(start, block)
        for n in range(3):
            fetched[2 + start // block * 3 + n].wait()
        grad = mlp_backward(
            up1[at, :], unit0_ref[at, :].astype(F32), whole(scale0_ref[at, :], width),
            slope0_ref[at, :],
            half_gain, up_ref[0], down_ref[0],
        )
        c0[start // half : start // half + 2] = grad.astype(BF16).reshape(2, half, width)
    taps0 = load_taps(k_ref, 0, True)

    def row0(i, carry):
        at = pl.ds(pl.multiple_of(i * half, half), half)
        bottom[at, :] = conv_row([c0[i + p].astype(F32) for p in range(3)], taps0).astype(BF16)
        return carry

    lax.fori_loop(0, patch_rows, row0, 0)
    fetched[-2].wait()
    fetched[-1].wait()
    for ab in range(4):
        part = mm_t(wp[ab], bottom[...])
        for i in range(patch_rows):
            at = ab * patch_rows + i
            mine = part[:, i * half : (i + 1) * half]
            full[at] = (gradt_ref[at].astype(F32) + mine).astype(BF16)
    split = lat_split(lat)
    for lon in range(lon_rows):
        i, a = lon // 2, lon % 2
        both = wide_dot([full[(2 * a + b) * patch_rows + i] for b in range(2)])
        put_lon_row(xf, lon, lon_rows, mm(both, split))
    sent = copies(
        [
            (xf.at[k, pl.ds(0, rows_out), :], out_hbm.at[:, pl.ds(k * 128, 128)])
            for k in range(lat // 128)
        ],
        out_sems,
    )
    for one in sent:
        one.wait()


ANY = pl.BlockSpec(memory_space=pl.ANY)
IN_VMEM = pl.BlockSpec(memory_space=pltpu.VMEM)
IN_SMEM = pl.BlockSpec(memory_space=pltpu.SMEM)


def call(kernel, outs, scratch, copies_in, copies_out, cost, smem=(), args=(), far=(), far_outs=(), limit=60):
    sems = [pltpu.SemaphoreType.DMA((n,)) for n in (copies_in, copies_out) if n]
    return pl.pallas_call(
        kernel,
        out_shape=[jax.ShapeDtypeStruct(shape, dtype) for shape, dtype in (*outs, *far_outs)],
        in_specs=[IN_SMEM] * len(smem) + [IN_VMEM] * len(args) + [ANY] * len(far),
        out_specs=[IN_VMEM] * len(outs) + [ANY] * len(far_outs),
        scratch_shapes=[pltpu.VMEM(shape, dtype) for shape, dtype in scratch] + sems,
        cost_estimate=pl.CostEstimate(
            flops=cost[0], bytes_accessed=cost[1], transcendentals=0
        ),
        compiler_params=pltpu.CompilerParams(vmem_limit_bytes=limit << 20),
    )(*smem, *args, *far)


def round_up(value, to):
    return -(-value // to) * to


BLOCK = 256


def shards(
    prior_state, patch_embed, conv_kernel, conv_bias, norm_gain, mlp_up, mlp_down, patch_unembed,
    emu_encode, chan_table, chan_head, head_bias, obs_cells, obs_chans, obs_values, obs_counts,
):
    lon_size = lax.axis_size("lon")
    lon_rows, chans, lat = prior_state.shape
    slots = obs_cells.shape[0]
    per_peer = slots // lon_size
    width = patch_embed.shape[3]
    hidden_size = mlp_up.shape[2]
    emu = emu_encode.shape[1]
    nchan = chan_table.shape[0]
    half, patch_rows = lat // 2, lon_rows // 2
    tokens, cells = half * patch_rows, lat * lon_rows
    wide = tokens + 2 * half
    head_pad = 32
    padded = round_up(chans + nchan, 256)
    packed = per_peer == BLOCK
    lanes = slots // 128
    state = jnp.transpose(prior_state, (1, 0, 2))
    u = jnp.transpose(patch_unembed, (1, 3, 2, 0))
    w = jnp.transpose(patch_embed, (0, 2, 1, 3))
    taps = jnp.transpose(conv_kernel, (1, 2, 0, 3))
    forward = [(i, (i + 1) % lon_size) for i in range(lon_size)]
    backward = [(target, source) for source, target in forward]

    halo = ((HALO * half, width), BF16)
    fat = ((wide, width), F32)
    fat_unit, thin_unit = ((wide, width), BF16), ((tokens, width), BF16)
    fat_scale, thin_scale = ((wide, 128), F32), ((tokens, 128), F32)
    fat_slope, thin_slope = ((wide, hidden_size), BF16), ((tokens, hidden_size), BF16)
    by_cell = ((cells // half, padded, half), BF16)
    rows_f32 = ((lat // 128, padded * lon_rows, 128), F32)
    maps = ((4, padded, width), BF16)
    lane_maps = ((width // 128, 2 * chans, 128), F32)
    maps_in = ((2, chans, 2, width), BF16)
    one_up, one_down = ((1, width, hidden_size), BF16), ((1, hidden_size, width), BF16)

    smem, args, outs = (), (), []
    if packed:
        smem = (obs_counts,)
        args = tuple(x.reshape(lanes, 128) for x in (obs_cells, obs_chans, obs_values))
        outs = [((lanes * 4, 128), F32)]
    hidden, first, last, *pay, xp, w = call(
        functools.partial(embed_kernel, lon_size if packed else None),
        [((tokens, width), BF16), halo, halo] + outs,
        [
            rows_f32, ((tokens, 4 * padded), BF16), maps, by_cell,
            ((chans, lon_rows, lat), BF16), maps_in, lane_maps,
        ],
        5, 2, (2 * tokens * 12 * padded * width, 4 * state.size),
        smem, args, (state, w), (by_cell, maps),
    )
    low = lax.ppermute(last, "lon", forward)
    high = lax.ppermute(first, "lon", backward)
    if packed:
        sent = pay[0].reshape(lon_size, 4 * per_peer // 128, 128)
    else:
        tile_lon, tile_lat = obs_cells // lat, obs_cells % lat
        place = (tile_lon % 2 * 2 + tile_lat % 2) * patch_rows + tile_lon // 2
        place = place * half + tile_lat // 2
        live = (jnp.arange(slots, dtype=jnp.int32) < obs_counts[0]).astype(F32)
        sent = jnp.stack(
            [
                part.astype(F32).reshape(lon_size, per_peer)
                for part in (place, obs_chans, obs_values, live)
            ],
            axis=1,
        )
    pay = lax.all_to_all(sent, "lon", split_axis=0, concat_axis=0, tiled=True)
    if not packed:
        group = BLOCK // per_peer
        pay = pay.reshape(lon_size // group, group, 4, per_peer)
        pay = jnp.transpose(pay, (0, 2, 1, 3)).reshape(lon_size // group, 8, 128)
    table, unit0, scale0, slope0, unit1, scale1, slope1, u = call(
        forward_kernel,
        [],
        [
            ((patch_rows + 2 * HALO, half, width), BF16),
            ((patch_rows + 2, half, width), BF16),
            fat,
            ((wide, width), BF16),
            ((tokens, width), BF16),
            maps, by_cell, maps_in,
            (mlp_up.shape, BF16), (mlp_down.shape, BF16),
            by_cell, fat_unit, fat_scale, fat_slope, thin_unit, thin_scale, thin_slope,
            lane_maps,
        ],
        4, 8, (3 * 10**9, 10**7),
        (), (hidden, low, high, taps, conv_bias, norm_gain), (xp, u, mlp_up, mlp_down),
        (by_cell, fat_unit, fat_scale, fat_slope, thin_unit, thin_scale, thin_slope, maps),
    )
    innov, grad, first, last, grad_t, denoised = call(
        radiance_kernel,
        [((lanes, 128), F32), ((tokens, width), BF16), halo, halo, by_cell],
        [
            ((emu // 128, padded, 128), BF16),
            ((padded // 128, emu, 128), BF16),
            ((emu // 128, head_pad, 128), BF16),
            ((emu, head_pad), BF16),
            ((lanes, half, 128), BF16),
            ((lanes, padded, 128), BF16),
            ((padded // 128, cells, 128), BF16),
            maps, rows_f32, ((chans, lon_rows, lat), BF16),
            ((padded, BLOCK), BF16), ((emu, BLOCK), GELU), ((emu, BLOCK), GELU),
            ((emu, BLOCK), BF16), ((emu, BLOCK), BF16),
            by_cell, one_up, one_down, thin_unit, thin_scale, thin_slope,
        ],
        7, 1, (14 * 10**9, 10**7),
        (),
        (pay, emu_encode, chan_table, chan_head, head_bias.reshape(1, nchan), norm_gain),
        (table, u, mlp_up, mlp_down, unit1, scale1, slope1),
        (((chans, lon_rows, lat), BF16),),
    )
    back = lax.ppermute(last, "lon", forward)
    ahead = lax.ppermute(first, "lon", backward)
    if packed:
        innov = innov.reshape(lon_size, per_peer // 128, 128)
    else:
        innov = innov.reshape(lon_size, per_peer)
    innovations = lax.all_to_all(innov, "lon", split_axis=0, concat_axis=0, tiled=True)
    (out,) = call(
        last_kernel,
        [],
        [
            ((patch_rows + 2 * HALO, half, width), BF16),
            fat,
            ((patch_rows + 2, half, width), BF16),
            ((tokens, width), BF16),
            by_cell, rows_f32, maps,
            fat_unit, fat_scale, fat_slope, by_cell, one_up, one_down,
        ],
        4 + 3 * (patch_rows + 2) // 2, lat // 128, (4 * 10**9, 10**7),
        (), (grad, back, ahead, taps, norm_gain),
        (unit0, scale0, slope0, grad_t, w, mlp_up, mlp_down),
        (((chans * lon_rows, lat), F32),),
    )
    state_gradient = jnp.transpose(out.reshape(chans, lon_rows, lat), (1, 0, 2))
    return (jnp.transpose(denoised, (1, 0, 2)), state_gradient, innovations.reshape(slots))


def solution(mesh):
    split = P(("groups", "lon"))
    placed = (split,) + (P(),) * 11 + (split,) * 4
    return jax.shard_map(
        shards, mesh=mesh, in_specs=placed, out_specs=(split,) * 3, check_vma=False
    )
```

time: 97.9 us -> 78.4 us (0.80)
  local copies, waits for them, and re-layouts: 9.72 us -> 2.61 us
  Pallas kernels: 56.6 us -> 50.3 us
  other arithmetic: 4.13 us -> 0 us
  starting transfers between devices: 16.3 us -> 13.7 us
    pallas_call x4, Pallas kernels: 56.6 us -> 50.3 us  [call(): pl.pallas_call(kernel, out_shape=[jax.ShapeDtypeStruct(shape, dtype) for...]
    all_to_all x1, starting transfers between devices: 7.41 us -> 3.62 us  [shards(): pay = lax.all_to_all(sent, 'lon', split_axis=0, concat_axis=0, tiled=True)]
    pad x3 -> x0, local copies, waits for them, and re-layouts: 2.33 us -> none  [the longest x1 0.85 us: shards(): u = jnp.pad(jnp.transpose(patch_unembed, (1, 2, 3, 0)), pad_c)]
    convert_element_type x3 -> x0, other arithmetic: 1.51 us -> none  [the longest x2 1.5 us: shards(): part.astype(F32).reshape(lon_size, per_peer)]
    another operation x1 -> x0, other arithmetic: 1.41 us -> none  [shards(): jnp.stack([part.astype(F32).reshape(lon_size, per_peer) for part in (plac...]
    unnamed x27 -> x11, local copies, waits for them, and re-layouts: 3.91 us -> 2.61 us
    concatenate x2 -> x0, local copies, waits for them, and re-layouts: 1.11 us -> none  [shards(): jnp.concatenate([emu_encode, chan_table, jnp.zeros((rest, emu), BF16)], a...]
    ppermute x1, starting transfers between devices: 4.03 us -> 5.05 us  [shards(): high = lax.ppermute(first, 'lon', backward)]
  transfers between devices with their start and end apart: 5 -> 5, of which waited for: 0 -> 0; matrix products, arithmetic and copies ran while one was open for 9% -> 0% of each run, Pallas kernels for 6% -> 10%
where the time goes in v2:
time: 78.4 us; the launch traced here: 78 us
  Pallas kernels  50.3 us (64%)
  starting transfers between devices  13.7 us (17%)
  blocking collectives  9.95 us (13%)
  local copies, waits for them, and re-layouts  2.61 us (3%)
  between operations  1.38 us (2%)
    pallas_call x4, Pallas kernels, call(): pl.pallas_call(kernel, out_shape=[jax.ShapeDtypeStruct(shape, dtype) for...  50.3 us
    all_to_all x1, blocking collectives, shards(): lax.all_to_all(innov, 'lon', split_axis=0, concat_axis=0, tiled=True)  9.95 us
    ppermute x1, starting transfers between devices, shards(): high = lax.ppermute(first, 'lon', backward)  5.05 us
    ppermute x1, starting transfers between devices, shards(): ahead = lax.ppermute(first, 'lon', backward)  4.03 us
    all_to_all x1, starting transfers between devices, shards(): pay = lax.all_to_all(sent, 'lon', split_axis=0, concat_axis=0, tiled=True)  3.62 us
    unnamed x11, local copies, waits for them, and re-layouts  2.61 us
  transfers between devices with their start and end apart: 5, of which 0 were waited for; matrix products, arithmetic and copies ran while one was open for 0% of the time, Pallas kernels for 10%

profile of v2, /device:TPU:0, one launch (start us, length us, event | category | flops | bytes accessed | tf_op | source)
XLA Modules:
  0.0 78.0 jit_solution(9749272074398629366)
XLA Ops:
  1.3 5.0 %shard_map.175 = (bf16[512,256]{1,0:T(8,128)(2,1)}, bf16[256,256]{1,0:T(8,128)(2,1)}, bf16[256,256]{1,0:T(8,128)(2,1)}, f32[128,128]{1,0:T(8,128)}, bf16[16,256,...) custom-call(s32[1]{0:T(128)S(6)} %copy.20.refs_0_, s32[32,128]{1,0:T(8,128)} %bitcast.21, s32[32,128]{1,0:T(8,128)} %bitcast.22, ...), custom_call_target="tpu_custom_call" | custom-call | flops 805306368 | bytes 1851392 | tf_op jit(solution)/shard_map/pallas_call | solution.py:531
  6.3 0.5 collective-permute-start
  6.8 5.0 %collective-permute-start.1 = (bf16[256,256]{1,0:T(8,128)(2,1)}, bf16[256,256]{1,0:T(8,128)(2,1)S(1)}, u32[]{:S(2)}, u32[]{:S(2)}) collective-permute-start(bf16[256,256]{1,0:T(8,128)(2,1)} %get-tuple-element.26), channel_id=1, source_target_pairs={{1,0},{2,1},{3,2},{4,3},{5,4},{6,5},{7,6},{8,7},{9,8},{10,9},{11,1... | collective-permute-start | bytes 393224 | tf_op jit(solution)/shard_map/ppermute | solution.py:605
  11.9 3.6 %all-to-all-start = ((f32[16,8,128]{2,1,0:T(8,128)}), f32[16,8,128]{2,1,0:T(8,128)S(1)}, u32[]{:S(2)}, u32[]{:S(2)}) async-start(f32[16,8,128]{2,1,0:T(8,128)} %bitcast.15), calls=%async_computation | async-start | bytes 131072 | tf_op jit(solution)/shard_map/all_to_all | solution.py:620
  15.5 0.0 collective-permute-done.lo_ref
  15.5 0.0 copy-start.1
  15.5 0.0 collective-permute-done.1.hi_ref
  15.5 0.0 copy-start.2
  15.5 0.6 copy-done.1
  16.2 0.1 copy-done.2
  16.2 8.0 %shard_map.176 = (bf16[16,256,128]{2,1,0:T(8,128)(2,1)}, bf16[768,256]{1,0:T(8,128)(2,1)}, f32[768,128]{1,0:T(8,128)}, bf16[768,1024]{1,0:T(8,128)(2,1)}, bf16[5...) custom-call(bf16[512,256]{1,0:T(8,128)(2,1)} %get-tuple-element.24.h_ref, ...), custom_call_target="tpu_custom_call" | custom-call | flops 3000000000 | bytes 10000000 | tf_op jit(solution)/shard_map/pallas_call | solution.py:531
  24.2 0.0 all-to-all-done.pay_ref
  24.2 0.0 copy-start
  24.2 0.6 copy-done
  24.8 29.8 %shard_map.177 = (f32[32,128]{1,0:T(8,128)}, bf16[512,256]{1,0:T(8,128)(2,1)}, bf16[256,256]{1,0:T(8,128)(2,1)}, bf16[256,256]{1,0:T(8,128)(2,1)}, bf16[16,256,1...) custom-call(f32[16,8,128]{2,1,0:T(8,128)} %copy-done, bf16[226,1024]{1,0:T(8,128)(2,1)} %enc_ref.1, ...), custom_call_target="tpu_custom_call" | custom-call | flops 14000000000 | bytes 10000000 | tf_op jit(solution)/shard_map/pallas_call | solution.py:531
  54.6 0.5 collective-permute-start.2
  55.1 4.0 %collective-permute-start.3 = (bf16[256,256]{1,0:T(8,128)(2,1)}, bf16[256,256]{1,0:T(8,128)(2,1)S(1)}, u32[]{:S(2)}, u32[]{:S(2)}) collective-permute-start(bf16[256,256]{1,0:T(8,128)(2,1)} %get-tuple-element.36), channel_id=1, source_target_pairs={{1,0},{2,1},{3,2},{4,3},{5,4},{6,5},{7,6},{8,7},{9,8},{10,9},{11,1... | collective-permute-start | bytes 393224 | tf_op jit(solution)/shard_map/ppermute | solution.py:666
  59.1 9.9 %all_to_all.10 = f32[16,2,128]{2,1,0:T(2,128)S(1)} all-to-all(f32[16,2,128]{2,1,0:T(2,128)} %bitcast.17), channel_id=1, replica_groups=mesh['groups'=2,'lon'=16] {'lon'}, dimensions={0} | all-to-all | bytes 32768 | tf_op jit(solution)/shard_map/all_to_all | solution.py:671
  69.0 0.0 collective-permute-done.2.lo_ref
  69.0 0.0 collective-permute-done.3.hi_ref
  69.1 0.6 copy-done.3
  69.7 0.1 copy-done.4
  69.8 7.6 %shard_map.178 = f32[1808,256]{1,0:T(8,128)} custom-call(bf16[512,256]{1,0:T(8,128)(2,1)} %get-tuple-element.34.cg_ref, bf16[256,256]{1,0:T(8,128)(2,1)} %copy-done.3, bf16[256,256]{1,0:T(8,128)(2,1)} %copy-done.4, bf16[3,3,2,256]{3,2,1,0:T(2,128)(2,1)} %bitcast.25, bf16[2,256]{1,0:T(2,128)(2,1)} %gain_ref.5, bf16[768,256]{1,0:T(8,128)(2,1)} %get-tuple-element.37.unit0_hbm, ...), custom_call_target="tpu_custom_call" | custom-call | flops 4000000000 | bytes 10000000 | tf_op jit(solution)/shard_map/pallas_call | solution.py:531
  77.4 0.6 copy.21
  (2 shorter events, 0.0 us)
Async XLA Ops:
  6.3 9.2 %collective-permute-start = (bf16[256,256]{1,0:T(8,128)(2,1)}, bf16[256,256]{1,0:T(8,128)(2,1)S(1)}, u32[]{:S(2)}, u32[]{:S(2)}) collective-permute-start(bf16[256,256]{1,0:T(8,128)(2,1)} %get-tuple-element.25), channel_id=1, source_target_pairs={{0,1},{1,2},{2,3},{3,4},{4,5},{5,6},{6,7},{7,8},{8,9},{9,10},{10,1... | collective-permute-start | bytes 393224 | tf_op jit(solution)/shard_map/ppermute | solution.py:604
  6.8 8.7 %collective-permute-start.1 = (bf16[256,256]{1,0:T(8,128)(2,1)}, bf16[256,256]{1,0:T(8,128)(2,1)S(1)}, u32[]{:S(2)}, u32[]{:S(2)}) collective-permute-start(bf16[256,256]{1,0:T(8,128)(2,1)} %get-tuple-element.26), channel_id=1, source_target_pairs={{1,0},{2,1},{3,2},{4,3},{5,4},{6,5},{7,6},{8,7},{9,8},{10,9},{11,1... | collective-permute-start | bytes 393224 | tf_op jit(solution)/shard_map/ppermute | solution.py:605
  11.9 12.3 %all-to-all-start = ((f32[16,8,128]{2,1,0:T(8,128)}), f32[16,8,128]{2,1,0:T(8,128)S(1)}, u32[]{:S(2)}, u32[]{:S(2)}) async-start(f32[16,8,128]{2,1,0:T(8,128)} %bitcast.15), calls=%async_computation | async-start | bytes 131072 | tf_op jit(solution)/shard_map/all_to_all | solution.py:620
  15.5 0.6 copy-start.1
  15.5 0.7 copy-start.2
  24.2 0.6 copy-start
  54.6 14.4 %collective-permute-start.2 = (bf16[256,256]{1,0:T(8,128)(2,1)}, bf16[256,256]{1,0:T(8,128)(2,1)S(1)}, u32[]{:S(2)}, u32[]{:S(2)}) collective-permute-start(bf16[256,256]{1,0:T(8,128)(2,1)} %get-tuple-element.35), channel_id=1, source_target_pairs={{0,1},{1,2},{2,3},{3,4},{4,5},{5,6},{6,7},{7,8},{8,9},{9,10},{10,1... | collective-permute-start | bytes 393224 | tf_op jit(solution)/shard_map/ppermute | solution.py:665
  55.1 14.0 %collective-permute-start.3 = (bf16[256,256]{1,0:T(8,128)(2,1)}, bf16[256,256]{1,0:T(8,128)(2,1)S(1)}, u32[]{:S(2)}, u32[]{:S(2)}) collective-permute-start(bf16[256,256]{1,0:T(8,128)(2,1)} %get-tuple-element.36), channel_id=1, source_target_pairs={{1,0},{2,1},{3,2},{4,3},{5,4},{6,5},{7,6},{8,7},{9,8},{10,9},{11,1... | collective-permute-start | bytes 393224 | tf_op jit(solution)/shard_map/ppermute | solution.py:666
  69.0 0.7 copy-start.3
  69.0 0.7 copy-start.4

commit v3 on v2

--- a/solution.py
+++ b/solution.py
@@ -107,9 +107,10 @@
     return jnp.concatenate(parts, axis=1)
 
 
-def put_lon_row(xf, lon, lon_rows, value):
+def put_lon_row(xf, lon, lon_rows, value, first=0):
     for k in range(xf.shape[0]):
-        xf[k, pl.ds(lon, value.shape[0], stride=lon_rows), :] = value[:, k * 128 : (k + 1) * 128]
+        at = pl.ds(first * lon_rows + lon, value.shape[0], stride=lon_rows)
+        xf[k, at, :] = value[:, k * 128 : (k + 1) * 128]
 
 
 def fill_weights(out, w_ref, lanes):
@@ -125,9 +126,7 @@
         out[ab, chans:, :] = jnp.zeros((out.shape[1] - chans, out.shape[2]), BF16)
 
 
-def embed_kernel(
-    peers, *refs
-):
+def embed_kernel(peers, fetch, ready, *refs):
     packed = peers is not None
     if packed:
         count_ref, cells_ref, chans_ref, values_ref, x_hbm, w_hbm = refs[:6]
@@ -141,33 +140,37 @@
     edges = [chans * n // 4 for n in range(5)]
     spans = [pl.ds(lo, hi - lo) for lo, hi in zip(edges, edges[1:])]
     fetched = copies([(x_hbm.at[at], x_ref.at[at]) for at in spans] + [(w_hbm, w_ref)], in_sems)
+    fetch()
     for k in range(lat // 128):
         xf[k, chans * lon_rows :, :] = jnp.zeros(((padded - chans) * lon_rows, 128), F32)
     for n in range(4):
         fetched[n].wait()
         fill_lanes(xf, x_ref, edges[n], edges[n + 1] - edges[n], lon_rows)
     split = lat_split(lat)
+    sent = []
     for lon in range(lon_rows):
         i, a = lon // 2, lon % 2
         rows = lon_row(xf, lon, lon_rows).astype(BF16)
         tokens = mm_t(split, rows).astype(BF16)
         part = mm_t(rows, split).astype(BF16)
         for b in range(2):
-            xp_ref[(2 * a + b) * (lon_rows // 2) + i] = part[:, b * half : (b + 1) * half]
+            place = (2 * a + b) * (lon_rows // 2) + i
+            xp_ref[place] = part[:, b * half : (b + 1) * half]
+            here = pl.ds(place, 1)
+            sent += copies([(xp_ref.at[here], xp_out.at[here])], sems.at[here])
             tcat[i * half : (i + 1) * half, (2 * a + b) * padded : (2 * a + b + 1) * padded] = tokens[
                 b * half : (b + 1) * half
             ]
     fetched[4].wait()
     fill_weights(wp, w_ref, lanes)
-    sent = copies([(xp_ref, xp_out), (wp, wp_out)], sems)
+    sent += copies([(wp, wp_out)], sems.at[pl.ds(2 * lon_rows, 1)])
     hidden = mm(tcat[...], wp[...].reshape(4 * padded, width)).astype(BF16)
     h_ref[...] = hidden
     first_ref[...] = hidden[: HALO * half]
     last_ref[...] = hidden[hidden.shape[0] - HALO * half :]
+    ready()
     if not packed:
-        for one in sent:
-            one.wait()
-        return
+        return sent
     rows, wide = cells_ref.shape
     per = rows // peers
     for part in range(per):
@@ -186,8 +189,7 @@
         kinds = (place.astype(F32), chans_ref[at, :].astype(F32), values_ref[at, :], live)
         for kind, value in enumerate(kinds):
             pay_ref[pl.ds(kind * per + part, peers, stride=4 * per), :] = value
-    for one in sent:
-        one.wait()
+    return sent
 
 
 def mlp_forward(layer, norm, conv, slope, up_ref, down_ref, store, tokens, block):
@@ -225,19 +227,32 @@
 
 
 def forward_kernel(
-    h_ref, lo_ref, hi_ref, k_ref, bias_ref, gain_ref, xp_hbm, u_hbm, up_hbm, down_hbm,
+    fetch, ready, h_ref, lo_ref, hi_ref, k_ref, bias_ref, gain_ref, xp_hbm, u_hbm, up_hbm, down_hbm,
     table_out, unit0_out, scale0_out, slope0_out, unit1_out, scale1_out, slope1_out, up_out,
     h0, h1, conv, norm, h2, up, xp_ref, u_ref, up_ref, down_ref,
     table_ref, unit0, scale0, slope0, unit1, scale1, slope1, lanes, sems, out_sems,
 ):
-    fetched = copies(
-        [(up_hbm, up_ref), (down_hbm, down_ref), (u_hbm, u_ref), (xp_hbm, xp_ref)], sems
+    fetch()
+    low, high = pl.ds(0, 1), pl.ds(1, 1)
+    early = copies(
+        [(up_hbm.at[low], up_ref.at[low]), (down_hbm.at[low], down_ref.at[low])],
+        sems.at[pl.ds(0, 2)],
     )
     _, _, half = table_ref.shape
     width = up.shape[2]
     tokens = h_ref.shape[0]
     patch_rows = tokens // half
     wide = (patch_rows + 2) * half
+    ready()
+    late = copies(
+        [
+            (u_hbm, u_ref),
+            (up_hbm.at[high], up_ref.at[high]),
+            (down_hbm.at[high], down_ref.at[high]),
+            (xp_hbm, xp_ref),
+        ],
+        sems.at[pl.ds(2, 4)],
+    )
     h0[0:HALO] = lo_ref[...].reshape(HALO, half, width)
     h0[HALO : HALO + patch_rows] = h_ref[...].reshape(patch_rows, half, width)
     h0[HALO + patch_rows :] = hi_ref[...].reshape(HALO, half, width)
@@ -248,13 +263,13 @@
     def to_h1(start, out):
         h1[start // half : (start + out.shape[0]) // half] = out.reshape(-1, half, width)
 
-    fetched[0].wait()
-    fetched[1].wait()
+    early[0].wait()
+    early[1].wait()
     mlp_forward(0, norm, conv, slope0, up_ref, down_ref, to_h1, wide, 2 * half)
     sent = copies(
         [(unit0, unit0_out), (scale0, scale0_out), (slope0, slope0_out)], out_sems.at[pl.ds(0, 3)]
     )
-    fetched[2].wait()
+    late[0].wait()
     fill_weights(up, u_ref, lanes)
     sent += copies([(up, up_out)], out_sems.at[pl.ds(7, 1)])
     conv_norm_rows(
@@ -264,20 +279,20 @@
     def to_h2(start, out):
         h2[start : start + out.shape[0], :] = out
 
+    late[1].wait()
+    late[2].wait()
     mlp_forward(1, norm, conv, slope1, up_ref, down_ref, to_h2, tokens, 2 * half)
     sent += copies(
         [(unit1, unit1_out), (scale1, scale1_out), (slope1, slope1_out)], out_sems.at[pl.ds(3, 3)]
     )
-    fetched[3].wait()
+    late[3].wait()
     for ab in range(4):
         part = mm_t(up[ab], h2[...])
         for i in range(patch_rows):
             at = ab * patch_rows + i
             mine = part[:, i * half : (i + 1) * half]
             table_ref[at] = (xp_ref[at].astype(F32) + mine).astype(BF16)
-    sent += copies([(table_ref, table_out)], out_sems.at[pl.ds(6, 1)])
-    for one in sent:
-        one.wait()
+    return sent + copies([(table_ref, table_out)], out_sems.at[pl.ds(6, 1)])
 
 
 def is_cell(key, high):
@@ -291,12 +306,13 @@
 
 
 def radiance_kernel(
-    pay_ref, enc_ref, tab_ref, head_ref, hbias_ref, gain_ref,
+    fetch, ready, pay_ref, enc_ref, tab_ref, head_ref, hbias_ref, gain_ref,
     table_hbm, u_hbm, up_hbm, down_hbm, unit1_hbm, scale1_hbm, slope1_hbm,
-    innov_ref, cg_ref, first_ref, last_ref, gradt_ref, den_out,
-    enc, enct, heads, headst, keys, gt, gcell, up, xf, den, inputs, pre, out, value, slope,
-    table_ref, up_ref, down_ref, unit1_ref, scale1_ref, slope1_ref, sems, out_sems,
+    innov_ref, cg_ref, first_ref, last_ref, gradt_out, den_out,
+    enc, enct, heads, headst, keys, gt, gcell, up, xf, den, inputs, pre, out, sums, slope,
+    table_ref, up_ref, down_ref, unit1_ref, scale1_ref, slope1_ref, gradt_ref, sems, out_sems,
 ):
+    fetch()
     fetched = copies(
         [
             (table_hbm, table_ref),
@@ -320,6 +336,7 @@
     one_at = round_up(chans, 8)
     tail = padded - heads.shape[1]
     shift = one_at - tail
+    ready()
     zeros = jnp.zeros((one_at - chans, 128), BF16)
     eye = identity(padded)
     for k in range(emu // 128):
@@ -331,12 +348,14 @@
         heads[k, 0:shift, :] = jnp.zeros((shift, 128), BF16)
         heads[k, shift : shift + nchan, :] = head_ref[:, cols]
         heads[k, shift + nchan :, :] = jnp.zeros((heads.shape[1] - shift - nchan, 128), BF16)
+    headst[...] = jnp.zeros_like(headst)
     for k in range(0, emu // 128, padded // 128):
         rows = slice(k * 128, k * 128 + padded)
         flip = mm_t(eye, wide_dot([enc[k + n] for n in range(padded // 128)])).astype(BF16)
         for n in range(padded // 128):
             enct[n, rows, :] = flip[:, n * 128 : (n + 1) * 128]
-        headst[rows, :] = mm_t(eye, wide_dot([heads[k + n] for n in range(padded // 128)])).astype(BF16)
+        flip = mm_t(eye, wide_dot([heads[k + n] for n in range(padded // 128)])).astype(F32)
+        headst[rows, 0:nchan] = flip[:, shift : shift + nchan]
     rows = heads.shape[1]
     spot = lax.broadcasted_iota(jnp.int32, (rows, nchan), 0)
     lane = lax.broadcasted_iota(jnp.int32, (rows, nchan), 1)
@@ -352,7 +371,7 @@
     for k in range(lat // 128):
         part = xf[k, 0 : chans * lon_rows, :].reshape(chans, lon_rows, 128)
         den[:, :, k * 128 : (k + 1) * 128] = part.astype(BF16)
-    sent = copies([(den, den_out)], out_sems)
+    sent = copies([(den, den_out)], out_sems.at[pl.ds(0, 1)])
 
     def row_of(pay, kind):
         return wide_dot([pay[2 * kind : 2 * kind + 1], pay[2 * kind + 1 : 2 * kind + 2]])
@@ -378,22 +397,32 @@
         inputs[tail:, :] = (columns[tail:] + one_hot).astype(BF16)
 
     def first_layer(p):
-        one_hot = one_hot_of(pay_ref[p])
         pre[...] = mm(wide_dot([enct[n] for n in range(padded // 128)]), inputs[...]).astype(GELU)
-        out[...] = mm(headst[:, 0:rows], one_hot.astype(BF16)).astype(GELU)
+        for n in range(2):
+            chan = pay_ref[p][2 + n : 3 + n].astype(jnp.int32)
+            at = jnp.broadcast_to(chan, headst.shape)
+            picked = jnp.take_along_axis(headst[...], at, axis=1, mode="promise_in_bounds")
+            out[:, n * 128 : (n + 1) * 128] = picked
 
     def activate():
-        for start in range(0, emu, 32):
-            at = pl.ds(start, 32)
-            act, tilt = gelu_pair(pre[at, :])
-            value[at, :] = act.astype(BF16)
-            slope[at, :] = (tilt * out[at, :]).astype(BF16)
+        chunk, group = 32, 4
+        total = None
+        for first in range(0, emu, chunk * group):
+            terms = None
+            for start in range(first, first + chunk * group, chunk):
+                at = pl.ds(start, chunk)
+                act, tilt = gelu_pair(pre[at, :])
+                head = out[at, :].astype(GELU)
+                slope[at, :] = (tilt * head).astype(BF16)
+                terms = act * head if terms is None else terms + act * head
+            terms = terms.astype(F32)
+            total = terms if total is None else total + terms
+        sums[...] = jnp.sum(total.reshape(chunk // 8, 8, block), axis=0)
 
     def finish(p):
         pay = pay_ref[p]
-        found = mm(wide_dot([heads[k] for k in range(emu // 128)]), value[...])
-        found = (0.5 * found + bias_col) * one_hot_of(pay)
-        predicted = jnp.sum(found, axis=0, keepdims=True)
+        bias = jnp.sum(bias_col * one_hot_of(pay), axis=0, keepdims=True)
+        predicted = 0.5 * jnp.sum(sums[...], axis=0, keepdims=True) + bias
         innov = row_of(pay, 3) * (predicted - row_of(pay, 2))
         grad = mm(wide_dot([enc[k] for k in range(emu // 128)]), slope[...])
         grad = (grad * (0.5 * innov)).astype(BF16)
@@ -401,37 +430,47 @@
             innov_ref[pl.ds(2 * p + n, 1), :] = innov[:, n * 128 : (n + 1) * 128]
             gt[2 * p + n] = grad[:, n * 128 : (n + 1) * 128]
 
-    def steps(p, carry):
-        finish(lax.rem(p + blocks - 3, blocks))
-        activate()
-        first_layer(jnp.clip(p - 1, 0, blocks - 1))
-        gather(jnp.minimum(p, blocks - 1))
-        return carry
-
-    lax.fori_loop(0, blocks + 3, steps, 0)
+    def step(p, least=0, most=4):
+        if most > 3:
+            finish(p - 3)
+        if least < 3 <= most:
+            activate()
+        if least < 2 <= most:
+            first_layer(p - 1)
+        if least < 1:
+            gather(p)
+
+    for p in range(3):
+        step(p, 0, p + 1)
+    lax.fori_loop(3, blocks, lambda p, carry: (step(p), carry)[1], 0)
+    for p in range(3):
+        step(blocks + p, p + 1, 4)
 
     lane_blocks = keys.shape[0]
+
+    count = 4
 
     def scatter(r, carry):
         key = wide_dot([keys[k] for k in range(lane_blocks)])
-        high = (2 * r).astype(F32)
+        high = (count * r).astype(F32)
         picks = []
-        for n in range(2):
+        for n in range(count):
             want = jnp.full((1, 1), high + n, F32).astype(BF16)
             picks.append(jnp.where(key == want, jnp.asarray(1, BF16), jnp.asarray(0, BF16)))
         lhs = jnp.concatenate(picks, axis=0)
-        out = mm_t(lhs, wide_dot([gt[k] for k in range(lane_blocks)])).astype(BF16)
-        at = pl.ds(pl.multiple_of(r * 2 * half, 2 * half), 2 * half)
+        total = mm_t(lhs, wide_dot([gt[k] for k in range(lane_blocks)])).astype(BF16)
+        at = pl.ds(pl.multiple_of(r * count * half, count * half), count * half)
         for n in range(padded // 128):
-            gcell[n, at, :] = out[:, n * 128 : (n + 1) * 128]
+            gcell[n, at, :] = total[:, n * 128 : (n + 1) * 128]
         return carry
 
-    lax.fori_loop(0, cell_blocks // 2, scatter, 0)
+    lax.fori_loop(0, cell_blocks // count, scatter, 0)
     for one in fetched[1:]:
         one.wait()
     flip = mm_t(eye, wide_dot([gcell[n] for n in range(padded // 128)])).astype(BF16)
     for k in range(cell_blocks):
         gradt_ref[k] = flip[:, k * half : (k + 1) * half]
+    sent += copies([(gradt_ref, gradt_out)], out_sems.at[pl.ds(1, 1)])
     upstream = None
     for ab in range(4):
         at = slice(ab * tokens, (ab + 1) * tokens)
@@ -444,27 +483,33 @@
     cg_ref[...] = grad
     first_ref[...] = grad[: HALO * half]
     last_ref[...] = grad[tokens - HALO * half :]
-    sent[0].wait()
+    return sent
 
 
 def last_kernel(
-    cg_ref, lo_ref, hi_ref, k_ref, gain_ref,
+    fetch, ready, cg_ref, lo_ref, hi_ref, k_ref, gain_ref,
     unit0_hbm, scale0_hbm, slope0_hbm, gradt_hbm, w_hbm, up_hbm, down_hbm, out_hbm,
     c1, up1, c0, bottom, full, xf, wp,
     unit0_ref, scale0_ref, slope0_ref, gradt_ref, up_ref, down_ref, sems, out_sems,
 ):
+    fetch()
     wide, block = up1.shape[0], 2 * c1.shape[1]
     kept = [(slope0_hbm, slope0_ref), (unit0_hbm, unit0_ref), (scale0_hbm, scale0_ref)]
-    pairs = [(down_hbm.at[pl.ds(0, 1)], down_ref), (up_hbm.at[pl.ds(0, 1)], up_ref)]
+    early = copies(
+        [(down_hbm.at[pl.ds(0, 1)], down_ref), (up_hbm.at[pl.ds(0, 1)], up_ref)], sems.at[pl.ds(0, 2)]
+    )
+    ready()
+    pairs = []
     for start in range(0, wide, block):
         pairs += [(src.at[pl.ds(start, block)], dst.at[pl.ds(start, block)]) for src, dst in kept]
-    fetched = copies(pairs + [(w_hbm, wp), (gradt_hbm, gradt_ref)], sems)
+    late = copies(pairs + [(w_hbm, wp), (gradt_hbm, gradt_ref)], sems.at[pl.ds(2, len(pairs) + 2)])
     rows_out, lat = out_hbm.shape
     half = lat // 2
-    _, width = wp.shape[1:]
+    padded, width = wp.shape[1:]
     tokens = cg_ref.shape[0]
     patch_rows = tokens // half
     lon_rows = 2 * patch_rows
+    chans = rows_out // lon_rows
     c1[0:HALO] = lo_ref[...].reshape(HALO, half, width)
     c1[HALO : HALO + patch_rows] = cg_ref[...].reshape(patch_rows, half, width)
     c1[HALO + patch_rows :] = hi_ref[...].reshape(HALO, half, width)
@@ -477,12 +522,12 @@
 
     lax.fori_loop(0, patch_rows + 2, row1, 0)
     half_gain = 0.5 * gain_ref[...].astype(F32)[0:1]
-    fetched[0].wait()
-    fetched[1].wait()
+    early[0].wait()
+    early[1].wait()
     for start in range(0, wide, block):
         at = pl.ds(start, block)
         for n in range(3):
-            fetched[2 + start // block * 3 + n].wait()
+            late[start // block * 3 + n].wait()
         grad = mlp_backward(
             up1[at, :], unit0_ref[at, :].astype(F32), whole(scale0_ref[at, :], width),
             slope0_ref[at, :],
@@ -497,8 +542,8 @@
         return carry
 
     lax.fori_loop(0, patch_rows, row0, 0)
-    fetched[-2].wait()
-    fetched[-1].wait()
+    late[-2].wait()
+    late[-1].wait()
     for ab in range(4):
         part = mm_t(wp[ab], bottom[...])
         for i in range(patch_rows):
@@ -506,38 +551,66 @@
             mine = part[:, i * half : (i + 1) * half]
             full[at] = (gradt_ref[at].astype(F32) + mine).astype(BF16)
     split = lat_split(lat)
-    for lon in range(lon_rows):
-        i, a = lon // 2, lon % 2
-        both = wide_dot([full[(2 * a + b) * patch_rows + i] for b in range(2)])
-        put_lon_row(xf, lon, lon_rows, mm(both, split))
-    sent = copies(
-        [
-            (xf.at[k, pl.ds(0, rows_out), :], out_hbm.at[:, pl.ds(k * 128, 128)])
-            for k in range(lat // 128)
-        ],
-        out_sems,
-    )
+    sent = []
+    spans = [(0, padded // 2), (padded // 2, chans)]
+    for n, (low, high) in enumerate(spans):
+        for lon in range(lon_rows):
+            i, a = lon // 2, lon % 2
+            both = wide_dot([full[(2 * a + b) * patch_rows + i, low : low + padded // 2] for b in range(2)])
+            put_lon_row(xf, lon, lon_rows, mm(both, split), low)
+        at = pl.ds(low * lon_rows, (high - low) * lon_rows)
+        sent += copies(
+            [(xf.at[k, at, :], out_hbm.at[at, pl.ds(k * 128, 128)]) for k in range(lat // 128)],
+            out_sems.at[pl.ds(n * (lat // 128), lat // 128)],
+        )
+    return sent
+
+
+ANY = pl.BlockSpec(memory_space=pl.ANY)
+IN_SMEM = pl.BlockSpec(memory_space=pltpu.SMEM)
+
+
+def whole_copies(kernel, counts, *refs):
+    parts, at = [], 0
+    for count in counts:
+        parts.append(refs[at : at + count])
+        at += count
+    smem, args, far, outs, far_outs, args_in, outs_in, scratch, arg_sems, out_sems = parts
+    fetched = []
+
+    def fetch():
+        if args:
+            fetched.extend(copies(list(zip(args, args_in)), arg_sems[0]))
+
+    def ready():
+        for one in fetched:
+            one.wait()
+
+    sent = kernel(fetch, ready, *smem, *args_in, *far, *outs_in, *far_outs, *scratch)
+    if outs:
+        sent = list(sent) + copies(list(zip(outs_in, outs)), out_sems[0])
     for one in sent:
         one.wait()
 
 
-ANY = pl.BlockSpec(memory_space=pl.ANY)
-IN_VMEM = pl.BlockSpec(memory_space=pltpu.VMEM)
-IN_SMEM = pl.BlockSpec(memory_space=pltpu.SMEM)
-
-
-def call(kernel, outs, scratch, copies_in, copies_out, cost, smem=(), args=(), far=(), far_outs=(), limit=60):
+def call(kernel, outs, scratch, copies_in, copies_out, cost, smem=(), args=(), far=(), far_outs=()):
     sems = [pltpu.SemaphoreType.DMA((n,)) for n in (copies_in, copies_out) if n]
+    own = [[pltpu.SemaphoreType.DMA((n,))] if n else [] for n in (len(args), len(outs))]
+    counts = (
+        len(smem), len(args), len(far), len(outs), len(far_outs), len(args), len(outs),
+        len(scratch) + len(sems), len(own[0]), len(own[1]),
+    )
+    held = [(arg.shape, arg.dtype) for arg in args] + list(outs) + list(scratch)
     return pl.pallas_call(
-        kernel,
+        functools.partial(whole_copies, kernel, counts),
         out_shape=[jax.ShapeDtypeStruct(shape, dtype) for shape, dtype in (*outs, *far_outs)],
-        in_specs=[IN_SMEM] * len(smem) + [IN_VMEM] * len(args) + [ANY] * len(far),
-        out_specs=[IN_VMEM] * len(outs) + [ANY] * len(far_outs),
-        scratch_shapes=[pltpu.VMEM(shape, dtype) for shape, dtype in scratch] + sems,
+        in_specs=[IN_SMEM] * len(smem) + [ANY] * (len(args) + len(far)),
+        out_specs=[ANY] * (len(outs) + len(far_outs)),
+        scratch_shapes=[pltpu.VMEM(shape, dtype) for shape, dtype in held] + sems + own[0] + own[1],
         cost_estimate=pl.CostEstimate(
             flops=cost[0], bytes_accessed=cost[1], transcendentals=0
         ),
-        compiler_params=pltpu.CompilerParams(vmem_limit_bytes=limit << 20),
+        compiler_params=pltpu.CompilerParams(vmem_limit_bytes=60 << 20),
     )(*smem, *args, *far)
 
 
@@ -598,7 +671,7 @@
             rows_f32, ((tokens, 4 * padded), BF16), maps, by_cell,
             ((chans, lon_rows, lat), BF16), maps_in, lane_maps,
         ],
-        5, 2, (2 * tokens * 12 * padded * width, 4 * state.size),
+        5, cells // half + 1, (2 * tokens * 12 * padded * width, 4 * state.size),
         smem, args, (state, w), (by_cell, maps),
     )
     low = lax.ppermute(last, "lon", forward)
@@ -636,31 +709,31 @@
             by_cell, fat_unit, fat_scale, fat_slope, thin_unit, thin_scale, thin_slope,
             lane_maps,
         ],
-        4, 8, (3 * 10**9, 10**7),
+        6, 8, (3 * 10**9, 10**7),
         (), (hidden, low, high, taps, conv_bias, norm_gain), (xp, u, mlp_up, mlp_down),
         (by_cell, fat_unit, fat_scale, fat_slope, thin_unit, thin_scale, thin_slope, maps),
     )
     innov, grad, first, last, grad_t, denoised = call(
         radiance_kernel,
-        [((lanes, 128), F32), ((tokens, width), BF16), halo, halo, by_cell],
+        [((lanes, 128), F32), ((tokens, width), BF16), halo, halo],
         [
             ((emu // 128, padded, 128), BF16),
             ((padded // 128, emu, 128), BF16),
             ((emu // 128, head_pad, 128), BF16),
-            ((emu, head_pad), BF16),
+            ((emu, 128), F32),
             ((lanes, half, 128), BF16),
             ((lanes, padded, 128), BF16),
             ((padded // 128, cells, 128), BF16),
             maps, rows_f32, ((chans, lon_rows, lat), BF16),
-            ((padded, BLOCK), BF16), ((emu, BLOCK), GELU), ((emu, BLOCK), GELU),
-            ((emu, BLOCK), BF16), ((emu, BLOCK), BF16),
-            by_cell, one_up, one_down, thin_unit, thin_scale, thin_slope,
+            ((padded, BLOCK), BF16), ((emu, BLOCK), GELU), ((emu, BLOCK), F32),
+            ((8, BLOCK), F32), ((emu, BLOCK), BF16),
+            by_cell, one_up, one_down, thin_unit, thin_scale, thin_slope, by_cell,
         ],
-        7, 1, (14 * 10**9, 10**7),
+        7, 2, (14 * 10**9, 10**7),
         (),
         (pay, emu_encode, chan_table, chan_head, head_bias.reshape(1, nchan), norm_gain),
         (table, u, mlp_up, mlp_down, unit1, scale1, slope1),
-        (((chans, lon_rows, lat), BF16),),
+        (by_cell, ((chans, lon_rows, lat), BF16)),
     )
     back = lax.ppermute(last, "lon", forward)
     ahead = lax.ppermute(first, "lon", backward)
@@ -680,7 +753,7 @@
             by_cell, rows_f32, maps,
             fat_unit, fat_scale, fat_slope, by_cell, one_up, one_down,
         ],
-        4 + 3 * (patch_rows + 2) // 2, lat // 128, (4 * 10**9, 10**7),
+        4 + 3 * (patch_rows + 2) // 2, 2 * (lat // 128), (4 * 10**9, 10**7),
         (), (grad, back, ahead, taps, norm_gain),
         (unit0, scale0, slope0, grad_t, w, mlp_up, mlp_down),
         (((chans * lon_rows, lat), F32),),

time: 78.4 us -> 72 us (0.918)
  Pallas kernels: 50.3 us -> 44.1 us
    pallas_call x4, Pallas kernels: 50.3 us -> 44.1 us  [call(): pl.pallas_call(functools.partial(whole_copies, kernel, counts), out_shape...]
  transfers between devices with their start and end apart: 5 -> 5, of which waited for: 0 -> 0; matrix products, arithmetic and copies ran while one was open for 0% -> 0% of each run, Pallas kernels for 10% -> 11%
where the time goes in v3:
time: 72 us; the launch traced here: 71.7 us
  Pallas kernels  44.1 us (61%)
  starting transfers between devices  13.7 us (19%)
  blocking collectives  9.95 us (14%)
  local copies, waits for them, and re-layouts  2.61 us (4%)
  between operations  1.38 us (2%)
    pallas_call x4, Pallas kernels, call(): pl.pallas_call(functools.partial(whole_copies, kernel, counts), out_shape...  44.1 us
    all_to_all x1, blocking collectives, shards(): lax.all_to_all(innov, 'lon', split_axis=0, concat_axis=0, tiled=True)  9.95 us
    ppermute x1, starting transfers between devices, shards(): high = lax.ppermute(first, 'lon', backward)  5.05 us
    ppermute x1, starting transfers between devices, shards(): ahead = lax.ppermute(first, 'lon', backward)  4.04 us
    all_to_all x1, starting transfers between devices, shards(): pay = lax.all_to_all(sent, 'lon', split_axis=0, concat_axis=0, tiled=True)  3.62 us
    unnamed x11, local copies, waits for them, and re-layouts  2.61 us
  transfers between devices with their start and end apart: 5, of which 0 were waited for; matrix products, arithmetic and copies ran while one was open for 0% of the time, Pallas kernels for 11%

profile of v3, /device:TPU:0, one launch (start us, length us, event | category | flops | bytes accessed | tf_op | source)
XLA Modules:
  0.0 71.7 jit_solution(4750952019685011576)
XLA Ops:
  1.3 4.0 %shard_map.175 = (bf16[512,256]{1,0:T(8,128)(2,1)}, bf16[256,256]{1,0:T(8,128)(2,1)}, bf16[256,256]{1,0:T(8,128)(2,1)}, f32[128,128]{1,0:T(8,128)}, bf16[16,256,...) custom-call(s32[1]{0:T(128)S(6)} %copy.20.refs_0_, s32[32,128]{1,0:T(8,128)} %bitcast.21, s32[32,128]{1,0:T(8,128)} %bitcast.22, ...), custom_call_target="tpu_custom_call" | custom-call | flops 805306368 | bytes 1851392 | tf_op jit(solution)/shard_map/pallas_call | solution.py:604
  5.3 0.5 collective-permute-start
  5.8 5.0 %collective-permute-start.1 = (bf16[256,256]{1,0:T(8,128)(2,1)}, bf16[256,256]{1,0:T(8,128)(2,1)S(1)}, u32[]{:S(2)}, u32[]{:S(2)}) collective-permute-start(bf16[256,256]{1,0:T(8,128)(2,1)} %get-tuple-element.26), channel_id=1, source_target_pairs={{1,0},{2,1},{3,2},{4,3},{5,4},{6,5},{7,6},{8,7},{9,8},{10,9},{11,1... | collective-permute-start | bytes 393224 | tf_op jit(solution)/shard_map/ppermute | solution.py:678
  10.9 3.6 %all-to-all-start = ((f32[16,8,128]{2,1,0:T(8,128)}), f32[16,8,128]{2,1,0:T(8,128)S(1)}, u32[]{:S(2)}, u32[]{:S(2)}) async-start(f32[16,8,128]{2,1,0:T(8,128)} %bitcast.15), calls=%async_computation | async-start | bytes 131072 | tf_op jit(solution)/shard_map/all_to_all | solution.py:693
  14.5 0.0 collective-permute-done.refs_1_
  14.5 0.0 copy-start.1
  14.5 0.0 collective-permute-done.1.refs_2_
  14.5 0.0 copy-start.2
  14.5 0.6 copy-done.1
  15.1 0.1 copy-done.2
  15.2 8.0 %shard_map.176 = (bf16[16,256,128]{2,1,0:T(8,128)(2,1)}, bf16[768,256]{1,0:T(8,128)(2,1)}, f32[768,128]{1,0:T(8,128)}, bf16[768,1024]{1,0:T(8,128)(2,1)}, bf16[5...) custom-call(bf16[512,256]{1,0:T(8,128)(2,1)} %get-tuple-element.24.refs_0_, ...), custom_call_target="tpu_custom_call" | custom-call | flops 3000000000 | bytes 10000000 | tf_op jit(solution)/shard_map/pallas_call | solution.py:604
  23.2 0.0 all-to-all-done.refs_0_
  23.2 0.6 copy-done
  23.9 24.8 %shard_map.177 = (f32[32,128]{1,0:T(8,128)}, bf16[512,256]{1,0:T(8,128)(2,1)}, bf16[256,256]{1,0:T(8,128)(2,1)}, bf16[256,256]{1,0:T(8,128)(2,1)}, bf16[16,256,1...) custom-call(f32[16,8,128]{2,1,0:T(8,128)} %copy-done, bf16[226,1024]{1,0:T(8,128)(2,1)} %refs_1_.1, ...), custom_call_target="tpu_custom_call" | custom-call | flops 14000000000 | bytes 10000000 | tf_op jit(solution)/shard_map/pallas_call | solution.py:604
  48.7 0.5 collective-permute-start.2
  49.1 4.0 %collective-permute-start.3 = (bf16[256,256]{1,0:T(8,128)(2,1)}, bf16[256,256]{1,0:T(8,128)(2,1)S(1)}, u32[]{:S(2)}, u32[]{:S(2)}) collective-permute-start(bf16[256,256]{1,0:T(8,128)(2,1)} %get-tuple-element.36), channel_id=1, source_target_pairs={{1,0},{2,1},{3,2},{4,3},{5,4},{6,5},{7,6},{8,7},{9,8},{10,9},{11,1... | collective-permute-start | bytes 393224 | tf_op jit(solution)/shard_map/ppermute | solution.py:739
  53.2 9.9 %all_to_all.10 = f32[16,2,128]{2,1,0:T(2,128)S(1)} all-to-all(f32[16,2,128]{2,1,0:T(2,128)} %bitcast.17), channel_id=1, replica_groups=mesh['groups'=2,'lon'=16] {'lon'}, dimensions={0} | all-to-all | bytes 32768 | tf_op jit(solution)/shard_map/all_to_all | solution.py:744
  63.1 0.0 collective-permute-done.2.refs_1_
  63.1 0.0 collective-permute-done.3.refs_2_
  63.1 0.0 copy-start.4
  63.2 0.6 copy-done.3
  63.8 0.1 copy-done.4
  63.8 7.3 %shard_map.178 = f32[1808,256]{1,0:T(8,128)} custom-call(bf16[512,256]{1,0:T(8,128)(2,1)} %get-tuple-element.34.refs_0_, bf16[256,256]{1,0:T(8,128)(2,1)} %copy-done.3, bf16[256,256]{1,0:T(8,128)(2,1)} %copy-done.4, bf16[3,3,2,256]{3,2,1,0:T(2,128)(2,1)} %bitcast.25, bf16[2,256]{1,0:T(2,128)(2,1)} %refs_4_.3, bf16[768,256]{1,0:T(8,128)(2,1)} %get-tuple-element.37.refs_5_, ...), custom_call_target="tpu_custom_call" | custom-call | flops 4000000000 | bytes 10000000 | tf_op jit(solution)/shard_map/pallas_call | solution.py:604
  71.1 0.6 copy.21
  (2 shorter events, 0.0 us)
Async XLA Ops:
  5.3 9.2 %collective-permute-start = (bf16[256,256]{1,0:T(8,128)(2,1)}, bf16[256,256]{1,0:T(8,128)(2,1)S(1)}, u32[]{:S(2)}, u32[]{:S(2)}) collective-permute-start(bf16[256,256]{1,0:T(8,128)(2,1)} %get-tuple-element.25), channel_id=1, source_target_pairs={{0,1},{1,2},{2,3},{3,4},{4,5},{5,6},{6,7},{7,8},{8,9},{9,10},{10,1... | collective-permute-start | bytes 393224 | tf_op jit(solution)/shard_map/ppermute | solution.py:677
  5.8 8.7 %collective-permute-start.1 = (bf16[256,256]{1,0:T(8,128)(2,1)}, bf16[256,256]{1,0:T(8,128)(2,1)S(1)}, u32[]{:S(2)}, u32[]{:S(2)}) collective-permute-start(bf16[256,256]{1,0:T(8,128)(2,1)} %get-tuple-element.26), channel_id=1, source_target_pairs={{1,0},{2,1},{3,2},{4,3},{5,4},{6,5},{7,6},{8,7},{9,8},{10,9},{11,1... | collective-permute-start | bytes 393224 | tf_op jit(solution)/shard_map/ppermute | solution.py:678
  10.9 12.4 %all-to-all-start = ((f32[16,8,128]{2,1,0:T(8,128)}), f32[16,8,128]{2,1,0:T(8,128)S(1)}, u32[]{:S(2)}, u32[]{:S(2)}) async-start(f32[16,8,128]{2,1,0:T(8,128)} %bitcast.15), calls=%async_computation | async-start | bytes 131072 | tf_op jit(solution)/shard_map/all_to_all | solution.py:693
  14.5 0.6 copy-start.1
  14.5 0.7 copy-start.2
  23.2 0.6 copy-start
  48.7 14.4 %collective-permute-start.2 = (bf16[256,256]{1,0:T(8,128)(2,1)}, bf16[256,256]{1,0:T(8,128)(2,1)S(1)}, u32[]{:S(2)}, u32[]{:S(2)}) collective-permute-start(bf16[256,256]{1,0:T(8,128)(2,1)} %get-tuple-element.35), channel_id=1, source_target_pairs={{0,1},{1,2},{2,3},{3,4},{4,5},{5,6},{6,7},{7,8},{8,9},{9,10},{10,1... | collective-permute-start | bytes 393224 | tf_op jit(solution)/shard_map/ppermute | solution.py:738
  49.1 14.0 %collective-permute-start.3 = (bf16[256,256]{1,0:T(8,128)(2,1)}, bf16[256,256]{1,0:T(8,128)(2,1)S(1)}, u32[]{:S(2)}, u32[]{:S(2)}) collective-permute-start(bf16[256,256]{1,0:T(8,128)(2,1)} %get-tuple-element.36), channel_id=1, source_target_pairs={{1,0},{2,1},{3,2},{4,3},{5,4},{6,5},{7,6},{8,7},{9,8},{10,9},{11,1... | collective-permute-start | bytes 393224 | tf_op jit(solution)/shard_map/ppermute | solution.py:739
  63.1 0.7 copy-start.3
  63.1 0.7 copy-start.4

commit v4 on v3

--- a/solution.py
+++ b/solution.py
@@ -313,18 +313,7 @@
     table_ref, up_ref, down_ref, unit1_ref, scale1_ref, slope1_ref, gradt_ref, sems, out_sems,
 ):
     fetch()
-    fetched = copies(
-        [
-            (table_hbm, table_ref),
-            (u_hbm, up),
-            (up_hbm.at[pl.ds(1, 1)], up_ref),
-            (down_hbm.at[pl.ds(1, 1)], down_ref),
-            (unit1_hbm, unit1_ref),
-            (scale1_hbm, scale1_ref),
-            (slope1_hbm, slope1_ref),
-        ],
-        sems,
-    )
+    (table_in,) = copies([(table_hbm, table_ref)], sems.at[pl.ds(0, 1)])
     chans, emu = enc_ref.shape
     nchan = tab_ref.shape[0]
     cell_blocks, padded, half = table_ref.shape
@@ -362,7 +351,18 @@
     bias_row = jnp.broadcast_to(hbias_ref[...], (rows, nchan))
     bias_col = jnp.sum(jnp.where(spot == lane + shift, bias_row, 0.0), axis=1, keepdims=True)
 
-    fetched[0].wait()
+    table_in.wait()
+    fetched = copies(
+        [
+            (u_hbm, up),
+            (up_hbm.at[pl.ds(1, 1)], up_ref),
+            (down_hbm.at[pl.ds(1, 1)], down_ref),
+            (unit1_hbm, unit1_ref),
+            (scale1_hbm, scale1_ref),
+            (slope1_hbm, slope1_ref),
+        ],
+        sems.at[pl.ds(1, 6)],
+    )
     split = lat_split(lat)
     for lon in range(lon_rows):
         i, a = lon // 2, lon % 2
@@ -465,7 +465,7 @@
         return carry
 
     lax.fori_loop(0, cell_blocks // count, scatter, 0)
-    for one in fetched[1:]:
+    for one in fetched:
         one.wait()
     flip = mm_t(eye, wide_dot([gcell[n] for n in range(padded // 128)])).astype(BF16)
     for k in range(cell_blocks):

time: 72 us -> 71.3 us (level)
  Pallas kernels: 44.1 us -> 43.3 us
    pallas_call x4, Pallas kernels: 44.1 us -> 43.3 us  [call(): pl.pallas_call(functools.partial(whole_copies, kernel, counts), out_shape...]
where the time goes in v4:
time: 71.3 us; the launch traced here: 71 us
  Pallas kernels  43.3 us (61%)
  starting transfers between devices  13.7 us (19%)
  blocking collectives  9.95 us (14%)
  local copies, waits for them, and re-layouts  2.61 us (4%)
  between operations  1.38 us (2%)
    pallas_call x4, Pallas kernels, call(): pl.pallas_call(functools.partial(whole_copies, kernel, counts), out_shape...  43.3 us
    all_to_all x1, blocking collectives, shards(): lax.all_to_all(innov, 'lon', split_axis=0, concat_axis=0, tiled=True)  9.95 us
    ppermute x1, starting transfers between devices, shards(): high = lax.ppermute(first, 'lon', backward)  5.05 us
    ppermute x1, starting transfers between devices, shards(): ahead = lax.ppermute(first, 'lon', backward)  4.04 us
    all_to_all x1, starting transfers between devices, shards(): pay = lax.all_to_all(sent, 'lon', split_axis=0, concat_axis=0, tiled=True)  3.62 us
    unnamed x11, local copies, waits for them, and re-layouts  2.61 us
  transfers between devices with their start and end apart: 5, of which 0 were waited for; matrix products, arithmetic and copies ran while one was open for 0% of the time, Pallas kernels for 11%

profile of v4, /device:TPU:0, one launch (start us, length us, event | category | flops | bytes accessed | tf_op | source)
XLA Modules:
  0.0 71.0 jit_solution(1189949622571995360)
XLA Ops:
  1.3 4.0 %shard_map.175 = (bf16[512,256]{1,0:T(8,128)(2,1)}, bf16[256,256]{1,0:T(8,128)(2,1)}, bf16[256,256]{1,0:T(8,128)(2,1)}, f32[128,128]{1,0:T(8,128)}, bf16[16,256,...) custom-call(s32[1]{0:T(128)S(6)} %copy.20.refs_0_, s32[32,128]{1,0:T(8,128)} %bitcast.21, s32[32,128]{1,0:T(8,128)} %bitcast.22, ...), custom_call_target="tpu_custom_call" | custom-call | flops 805306368 | bytes 1851392 | tf_op jit(solution)/shard_map/pallas_call | solution.py:604
  5.3 0.5 collective-permute-start
  5.8 5.0 %collective-permute-start.1 = (bf16[256,256]{1,0:T(8,128)(2,1)}, bf16[256,256]{1,0:T(8,128)(2,1)S(1)}, u32[]{:S(2)}, u32[]{:S(2)}) collective-permute-start(bf16[256,256]{1,0:T(8,128)(2,1)} %get-tuple-element.26), channel_id=1, source_target_pairs={{1,0},{2,1},{3,2},{4,3},{5,4},{6,5},{7,6},{8,7},{9,8},{10,9},{11,1... | collective-permute-start | bytes 393224 | tf_op jit(solution)/shard_map/ppermute | solution.py:678
  10.9 3.6 %all-to-all-start = ((f32[16,8,128]{2,1,0:T(8,128)}), f32[16,8,128]{2,1,0:T(8,128)S(1)}, u32[]{:S(2)}, u32[]{:S(2)}) async-start(f32[16,8,128]{2,1,0:T(8,128)} %bitcast.15), calls=%async_computation | async-start | bytes 131072 | tf_op jit(solution)/shard_map/all_to_all | solution.py:693
  14.5 0.0 collective-permute-done.refs_1_
  14.5 0.0 copy-start.1
  14.5 0.0 collective-permute-done.1.refs_2_
  14.5 0.0 copy-start.2
  14.5 0.6 copy-done.1
  15.1 0.1 copy-done.2
  15.2 8.0 %shard_map.176 = (bf16[16,256,128]{2,1,0:T(8,128)(2,1)}, bf16[768,256]{1,0:T(8,128)(2,1)}, f32[768,128]{1,0:T(8,128)}, bf16[768,1024]{1,0:T(8,128)(2,1)}, bf16[5...) custom-call(bf16[512,256]{1,0:T(8,128)(2,1)} %get-tuple-element.24.refs_0_, ...), custom_call_target="tpu_custom_call" | custom-call | flops 3000000000 | bytes 10000000 | tf_op jit(solution)/shard_map/pallas_call | solution.py:604
  23.2 0.0 all-to-all-done.refs_0_
  23.2 0.0 copy-start
  23.2 0.6 copy-done
  23.9 24.1 %shard_map.177 = (f32[32,128]{1,0:T(8,128)}, bf16[512,256]{1,0:T(8,128)(2,1)}, bf16[256,256]{1,0:T(8,128)(2,1)}, bf16[256,256]{1,0:T(8,128)(2,1)}, bf16[16,256,1...) custom-call(f32[16,8,128]{2,1,0:T(8,128)} %copy-done, bf16[226,1024]{1,0:T(8,128)(2,1)} %refs_1_.1, ...), custom_call_target="tpu_custom_call" | custom-call | flops 14000000000 | bytes 10000000 | tf_op jit(solution)/shard_map/pallas_call | solution.py:604
  47.9 0.5 collective-permute-start.2
  48.4 4.0 %collective-permute-start.3 = (bf16[256,256]{1,0:T(8,128)(2,1)}, bf16[256,256]{1,0:T(8,128)(2,1)S(1)}, u32[]{:S(2)}, u32[]{:S(2)}) collective-permute-start(bf16[256,256]{1,0:T(8,128)(2,1)} %get-tuple-element.36), channel_id=1, source_target_pairs={{1,0},{2,1},{3,2},{4,3},{5,4},{6,5},{7,6},{8,7},{9,8},{10,9},{11,1... | collective-permute-start | bytes 393224 | tf_op jit(solution)/shard_map/ppermute | solution.py:739
  52.4 9.9 %all_to_all.10 = f32[16,2,128]{2,1,0:T(2,128)S(1)} all-to-all(f32[16,2,128]{2,1,0:T(2,128)} %bitcast.17), channel_id=1, replica_groups=mesh['groups'=2,'lon'=16] {'lon'}, dimensions={0} | all-to-all | bytes 32768 | tf_op jit(solution)/shard_map/all_to_all | solution.py:744
  62.4 0.0 collective-permute-done.2.refs_1_
  62.4 0.0 collective-permute-done.3.refs_2_
  62.4 0.6 copy-done.3
  63.0 0.1 copy-done.4
  63.1 7.3 %shard_map.178 = f32[1808,256]{1,0:T(8,128)} custom-call(bf16[512,256]{1,0:T(8,128)(2,1)} %get-tuple-element.34.refs_0_, bf16[256,256]{1,0:T(8,128)(2,1)} %copy-done.3, bf16[256,256]{1,0:T(8,128)(2,1)} %copy-done.4, bf16[3,3,2,256]{3,2,1,0:T(2,128)(2,1)} %bitcast.25, bf16[2,256]{1,0:T(2,128)(2,1)} %refs_4_.3, bf16[768,256]{1,0:T(8,128)(2,1)} %get-tuple-element.37.refs_5_, ...), custom_call_target="tpu_custom_call" | custom-call | flops 4000000000 | bytes 10000000 | tf_op jit(solution)/shard_map/pallas_call | solution.py:604
  70.3 0.6 copy.21
  (2 shorter events, 0.0 us)
Async XLA Ops:
  5.3 9.2 %collective-permute-start = (bf16[256,256]{1,0:T(8,128)(2,1)}, bf16[256,256]{1,0:T(8,128)(2,1)S(1)}, u32[]{:S(2)}, u32[]{:S(2)}) collective-permute-start(bf16[256,256]{1,0:T(8,128)(2,1)} %get-tuple-element.25), channel_id=1, source_target_pairs={{0,1},{1,2},{2,3},{3,4},{4,5},{5,6},{6,7},{7,8},{8,9},{9,10},{10,1... | collective-permute-start | bytes 393224 | tf_op jit(solution)/shard_map/ppermute | solution.py:677
  5.8 8.7 %collective-permute-start.1 = (bf16[256,256]{1,0:T(8,128)(2,1)}, bf16[256,256]{1,0:T(8,128)(2,1)S(1)}, u32[]{:S(2)}, u32[]{:S(2)}) collective-permute-start(bf16[256,256]{1,0:T(8,128)(2,1)} %get-tuple-element.26), channel_id=1, source_target_pairs={{1,0},{2,1},{3,2},{4,3},{5,4},{6,5},{7,6},{8,7},{9,8},{10,9},{11,1... | collective-permute-start | bytes 393224 | tf_op jit(solution)/shard_map/ppermute | solution.py:678
  10.9 12.4 %all-to-all-start = ((f32[16,8,128]{2,1,0:T(8,128)}), f32[16,8,128]{2,1,0:T(8,128)S(1)}, u32[]{:S(2)}, u32[]{:S(2)}) async-start(f32[16,8,128]{2,1,0:T(8,128)} %bitcast.15), calls=%async_computation | async-start | bytes 131072 | tf_op jit(solution)/shard_map/all_to_all | solution.py:693
  14.5 0.6 copy-start.1
  14.5 0.7 copy-start.2
  23.2 0.6 copy-start
  47.9 14.4 %collective-permute-start.2 = (bf16[256,256]{1,0:T(8,128)(2,1)}, bf16[256,256]{1,0:T(8,128)(2,1)S(1)}, u32[]{:S(2)}, u32[]{:S(2)}) collective-permute-start(bf16[256,256]{1,0:T(8,128)(2,1)} %get-tuple-element.35), channel_id=1, source_target_pairs={{0,1},{1,2},{2,3},{3,4},{4,5},{5,6},{6,7},{7,8},{8,9},{9,10},{10,1... | collective-permute-start | bytes 393224 | tf_op jit(solution)/shard_map/ppermute | solution.py:738
  48.4 14.0 %collective-permute-start.3 = (bf16[256,256]{1,0:T(8,128)(2,1)}, bf16[256,256]{1,0:T(8,128)(2,1)S(1)}, u32[]{:S(2)}, u32[]{:S(2)}) collective-permute-start(bf16[256,256]{1,0:T(8,128)(2,1)} %get-tuple-element.36), channel_id=1, source_target_pairs={{1,0},{2,1},{3,2},{4,3},{5,4},{6,5},{7,6},{8,7},{9,8},{10,9},{11,1... | collective-permute-start | bytes 393224 | tf_op jit(solution)/shard_map/ppermute | solution.py:739
  62.4 0.7 copy-start.3
  62.4 0.7 copy-start.4

commit v5 on v4

--- a/solution.py
+++ b/solution.py
@@ -217,7 +217,7 @@
         norm[at, :] = (u * gain).astype(BF16)
         return carry
 
-    lax.fori_loop(0, count, row, 0)
+    lax.fori_loop(0, count, row, 0, unroll=True)
 
 
 def mlp_backward(upstream, unit, scale, slope, half_gain, up, down):
@@ -271,7 +271,7 @@
     )
     late[0].wait()
     fill_weights(up, u_ref, lanes)
-    sent += copies([(up, up_out)], out_sems.at[pl.ds(7, 1)])
+    sent += copies([(up, up_out)], out_sems.at[pl.ds(6, 1)])
     conv_norm_rows(
         patch_rows, h1, 1, k_ref, bias_ref, gain_ref, conv, unit1, scale1, norm, half
     )
@@ -288,11 +288,13 @@
     late[3].wait()
     for ab in range(4):
         part = mm_t(up[ab], h2[...])
+        here = pl.ds(ab * patch_rows, patch_rows)
         for i in range(patch_rows):
             at = ab * patch_rows + i
             mine = part[:, i * half : (i + 1) * half]
             table_ref[at] = (xp_ref[at].astype(F32) + mine).astype(BF16)
-    return sent + copies([(table_ref, table_out)], out_sems.at[pl.ds(6, 1)])
+        sent += copies([(table_ref.at[here], table_out.at[here])], out_sems.at[pl.ds(7 + ab, 1)])
+    return sent
 
 
 def is_cell(key, high):
@@ -363,15 +365,6 @@
         ],
         sems.at[pl.ds(1, 6)],
     )
-    split = lat_split(lat)
-    for lon in range(lon_rows):
-        i, a = lon // 2, lon % 2
-        both = wide_dot([table_ref[(2 * a + b) * patch_rows + i] for b in range(2)])
-        put_lon_row(xf, lon, lon_rows, mm(both, split))
-    for k in range(lat // 128):
-        part = xf[k, 0 : chans * lon_rows, :].reshape(chans, lon_rows, 128)
-        den[:, :, k * 128 : (k + 1) * 128] = part.astype(BF16)
-    sent = copies([(den, den_out)], out_sems.at[pl.ds(0, 1)])
 
     def row_of(pay, kind):
         return wide_dot([pay[2 * kind : 2 * kind + 1], pay[2 * kind + 1 : 2 * kind + 2]])
@@ -443,12 +436,21 @@
     for p in range(3):
         step(p, 0, p + 1)
     lax.fori_loop(3, blocks, lambda p, carry: (step(p), carry)[1], 0)
+    split = lat_split(lat)
+    for lon in range(lon_rows):
+        i, a = lon // 2, lon % 2
+        both = wide_dot([table_ref[(2 * a + b) * patch_rows + i] for b in range(2)])
+        put_lon_row(xf, lon, lon_rows, mm(both, split))
+    for k in range(lat // 128):
+        part = xf[k, 0 : chans * lon_rows, :].reshape(chans, lon_rows, 128)
+        den[:, :, k * 128 : (k + 1) * 128] = part.astype(BF16)
+    sent = copies([(den, den_out)], out_sems.at[pl.ds(0, 1)])
     for p in range(3):
         step(blocks + p, p + 1, 4)
 
     lane_blocks = keys.shape[0]
 
-    count = 4
+    count = 8
 
     def scatter(r, carry):
         key = wide_dot([keys[k] for k in range(lane_blocks)])
@@ -520,7 +522,7 @@
         up1[at, :] = conv_row([c1[i + p].astype(F32) for p in range(3)], taps)
         return carry
 
-    lax.fori_loop(0, patch_rows + 2, row1, 0)
+    lax.fori_loop(0, patch_rows + 2, row1, 0, unroll=True)
     half_gain = 0.5 * gain_ref[...].astype(F32)[0:1]
     early[0].wait()
     early[1].wait()
@@ -541,7 +543,7 @@
         bottom[at, :] = conv_row([c0[i + p].astype(F32) for p in range(3)], taps0).astype(BF16)
         return carry
 
-    lax.fori_loop(0, patch_rows, row0, 0)
+    lax.fori_loop(0, patch_rows, row0, 0, unroll=True)
     late[-2].wait()
     late[-1].wait()
     for ab in range(4):
@@ -709,7 +711,7 @@
             by_cell, fat_unit, fat_scale, fat_slope, thin_unit, thin_scale, thin_slope,
             lane_maps,
         ],
-        6, 8, (3 * 10**9, 10**7),
+        6, 11, (3 * 10**9, 10**7),
         (), (hidden, low, high, taps, conv_bias, norm_gain), (xp, u, mlp_up, mlp_down),
         (by_cell, fat_unit, fat_scale, fat_slope, thin_unit, thin_scale, thin_slope, maps),
     )

time: 71.3 us -> 69.6 us (0.976)
  Pallas kernels: 43.3 us -> 41.6 us
    pallas_call x4, Pallas kernels: 43.3 us -> 41.6 us  [call(): pl.pallas_call(functools.partial(whole_copies, kernel, counts), out_shape...]
  transfers between devices with their start and end apart: 5 -> 5, of which waited for: 0 -> 0; matrix products, arithmetic and copies ran while one was open for 0% -> 0% of each run, Pallas kernels for 11% -> 10%
where the time goes in v5:
time: 69.6 us; the launch traced here: 69.2 us
  Pallas kernels  41.6 us (60%)
  starting transfers between devices  13.7 us (20%)
  blocking collectives  9.95 us (14%)
  local copies, waits for them, and re-layouts  2.61 us (4%)
  between operations  1.38 us (2%)
    pallas_call x4, Pallas kernels, call(): pl.pallas_call(functools.partial(whole_copies, kernel, counts), out_shape...  41.6 us
    all_to_all x1, blocking collectives, shards(): lax.all_to_all(innov, 'lon', split_axis=0, concat_axis=0, tiled=True)  9.95 us
    ppermute x1, starting transfers between devices, shards(): high = lax.ppermute(first, 'lon', backward)  5.05 us
    ppermute x1, starting transfers between devices, shards(): ahead = lax.ppermute(first, 'lon', backward)  4.03 us
    all_to_all x1, starting transfers between devices, shards(): pay = lax.all_to_all(sent, 'lon', split_axis=0, concat_axis=0, tiled=True)  3.62 us
    unnamed x11, local copies, waits for them, and re-layouts  2.61 us
  transfers between devices with their start and end apart: 5, of which 0 were waited for; matrix products, arithmetic and copies ran while one was open for 0% of the time, Pallas kernels for 10%

profile of v5, /device:TPU:0, one launch (start us, length us, event | category | flops | bytes accessed | tf_op | source)
XLA Modules:
  0.0 69.2 jit_solution(12791149831846125024)
XLA Ops:
  1.3 4.0 %shard_map.175 = (bf16[512,256]{1,0:T(8,128)(2,1)}, bf16[256,256]{1,0:T(8,128)(2,1)}, bf16[256,256]{1,0:T(8,128)(2,1)}, f32[128,128]{1,0:T(8,128)}, bf16[16,256,...) custom-call(s32[1]{0:T(128)S(6)} %copy.20.refs_0_, s32[32,128]{1,0:T(8,128)} %bitcast.21, s32[32,128]{1,0:T(8,128)} %bitcast.22, ...), custom_call_target="tpu_custom_call" | custom-call | flops 805306368 | bytes 1851392 | tf_op jit(solution)/shard_map/pallas_call | solution.py:606
  5.3 0.5 collective-permute-start
  5.8 5.0 %collective-permute-start.1 = (bf16[256,256]{1,0:T(8,128)(2,1)}, bf16[256,256]{1,0:T(8,128)(2,1)S(1)}, u32[]{:S(2)}, u32[]{:S(2)}) collective-permute-start(bf16[256,256]{1,0:T(8,128)(2,1)} %get-tuple-element.26), channel_id=1, source_target_pairs={{1,0},{2,1},{3,2},{4,3},{5,4},{6,5},{7,6},{8,7},{9,8},{10,9},{11,1... | collective-permute-start | bytes 393224 | tf_op jit(solution)/shard_map/ppermute | solution.py:680
  10.9 3.6 %all-to-all-start = ((f32[16,8,128]{2,1,0:T(8,128)}), f32[16,8,128]{2,1,0:T(8,128)S(1)}, u32[]{:S(2)}, u32[]{:S(2)}) async-start(f32[16,8,128]{2,1,0:T(8,128)} %bitcast.15), calls=%async_computation | async-start | bytes 131072 | tf_op jit(solution)/shard_map/all_to_all | solution.py:695
  14.5 0.0 collective-permute-done.refs_1_
  14.5 0.0 copy-start.1
  14.5 0.0 collective-permute-done.1.refs_2_
  14.5 0.0 copy-start.2
  14.5 0.6 copy-done.1
  15.1 0.1 copy-done.2
  15.2 6.7 %shard_map.176 = (bf16[16,256,128]{2,1,0:T(8,128)(2,1)}, bf16[768,256]{1,0:T(8,128)(2,1)}, f32[768,128]{1,0:T(8,128)}, bf16[768,1024]{1,0:T(8,128)(2,1)}, bf16[5...) custom-call(bf16[512,256]{1,0:T(8,128)(2,1)} %get-tuple-element.24.refs_0_, ...), custom_call_target="tpu_custom_call" | custom-call | flops 3000000000 | bytes 10000000 | tf_op jit(solution)/shard_map/pallas_call | solution.py:606
  21.9 0.0 all-to-all-done.refs_0_
  21.9 0.0 copy-start
  21.9 0.6 copy-done
  22.5 23.8 %shard_map.177 = (f32[32,128]{1,0:T(8,128)}, bf16[512,256]{1,0:T(8,128)(2,1)}, bf16[256,256]{1,0:T(8,128)(2,1)}, bf16[256,256]{1,0:T(8,128)(2,1)}, bf16[16,256,1...) custom-call(f32[16,8,128]{2,1,0:T(8,128)} %copy-done, bf16[226,1024]{1,0:T(8,128)(2,1)} %refs_1_.1, ...), custom_call_target="tpu_custom_call" | custom-call | flops 14000000000 | bytes 10000000 | tf_op jit(solution)/shard_map/pallas_call | solution.py:606
  46.3 0.5 collective-permute-start.2
  46.8 4.0 %collective-permute-start.3 = (bf16[256,256]{1,0:T(8,128)(2,1)}, bf16[256,256]{1,0:T(8,128)(2,1)S(1)}, u32[]{:S(2)}, u32[]{:S(2)}) collective-permute-start(bf16[256,256]{1,0:T(8,128)(2,1)} %get-tuple-element.36), channel_id=1, source_target_pairs={{1,0},{2,1},{3,2},{4,3},{5,4},{6,5},{7,6},{8,7},{9,8},{10,9},{11,1... | collective-permute-start | bytes 393224 | tf_op jit(solution)/shard_map/ppermute | solution.py:741
  50.8 9.9 %all_to_all.10 = f32[16,2,128]{2,1,0:T(2,128)S(1)} all-to-all(f32[16,2,128]{2,1,0:T(2,128)} %bitcast.17), channel_id=1, replica_groups=mesh['groups'=2,'lon'=16] {'lon'}, dimensions={0} | all-to-all | bytes 32768 | tf_op jit(solution)/shard_map/all_to_all | solution.py:746
  60.8 0.0 collective-permute-done.2.refs_1_
  60.8 0.0 collective-permute-done.3.refs_2_
  60.8 0.6 copy-done.3
  61.4 0.1 copy-done.4
  61.5 7.1 %shard_map.178 = f32[1808,256]{1,0:T(8,128)} custom-call(bf16[512,256]{1,0:T(8,128)(2,1)} %get-tuple-element.34.refs_0_, bf16[256,256]{1,0:T(8,128)(2,1)} %copy-done.3, bf16[256,256]{1,0:T(8,128)(2,1)} %copy-done.4, bf16[3,3,2,256]{3,2,1,0:T(2,128)(2,1)} %bitcast.25, bf16[2,256]{1,0:T(2,128)(2,1)} %refs_4_.3, bf16[768,256]{1,0:T(8,128)(2,1)} %get-tuple-element.37.refs_5_, ...), custom_call_target="tpu_custom_call" | custom-call | flops 4000000000 | bytes 10000000 | tf_op jit(solution)/shard_map/pallas_call | solution.py:606
  68.6 0.6 copy.21
  (2 shorter events, 0.0 us)
Async XLA Ops:
  5.3 9.2 %collective-permute-start = (bf16[256,256]{1,0:T(8,128)(2,1)}, bf16[256,256]{1,0:T(8,128)(2,1)S(1)}, u32[]{:S(2)}, u32[]{:S(2)}) collective-permute-start(bf16[256,256]{1,0:T(8,128)(2,1)} %get-tuple-element.25), channel_id=1, source_target_pairs={{0,1},{1,2},{2,3},{3,4},{4,5},{5,6},{6,7},{7,8},{8,9},{9,10},{10,1... | collective-permute-start | bytes 393224 | tf_op jit(solution)/shard_map/ppermute | solution.py:679
  5.8 8.7 %collective-permute-start.1 = (bf16[256,256]{1,0:T(8,128)(2,1)}, bf16[256,256]{1,0:T(8,128)(2,1)S(1)}, u32[]{:S(2)}, u32[]{:S(2)}) collective-permute-start(bf16[256,256]{1,0:T(8,128)(2,1)} %get-tuple-element.26), channel_id=1, source_target_pairs={{1,0},{2,1},{3,2},{4,3},{5,4},{6,5},{7,6},{8,7},{9,8},{10,9},{11,1... | collective-permute-start | bytes 393224 | tf_op jit(solution)/shard_map/ppermute | solution.py:680
  10.9 11.0 %all-to-all-start = ((f32[16,8,128]{2,1,0:T(8,128)}), f32[16,8,128]{2,1,0:T(8,128)S(1)}, u32[]{:S(2)}, u32[]{:S(2)}) async-start(f32[16,8,128]{2,1,0:T(8,128)} %bitcast.15), calls=%async_computation | async-start | bytes 131072 | tf_op jit(solution)/shard_map/all_to_all | solution.py:695
  14.5 0.6 copy-start.1
  14.5 0.7 %copy-start.2 = (bf16[256,256]{1,0:T(8,128)(2,1)}, bf16[256,256]{1,0:T(8,128)(2,1)S(1)}, u32[]{:S(2)}) copy-start(bf16[256,256]{1,0:T(8,128)(2,1)S(1)} %collective-permute-done.1.refs_2_) | copy-start | bytes 393220
  21.9 0.6 copy-start
  46.3 14.4 %collective-permute-start.2 = (bf16[256,256]{1,0:T(8,128)(2,1)}, bf16[256,256]{1,0:T(8,128)(2,1)S(1)}, u32[]{:S(2)}, u32[]{:S(2)}) collective-permute-start(bf16[256,256]{1,0:T(8,128)(2,1)} %get-tuple-element.35), channel_id=1, source_target_pairs={{0,1},{1,2},{2,3},{3,4},{4,5},{5,6},{6,7},{7,8},{8,9},{9,10},{10,1... | collective-permute-start | bytes 393224 | tf_op jit(solution)/shard_map/ppermute | solution.py:740
  46.8 14.0 %collective-permute-start.3 = (bf16[256,256]{1,0:T(8,128)(2,1)}, bf16[256,256]{1,0:T(8,128)(2,1)S(1)}, u32[]{:S(2)}, u32[]{:S(2)}) collective-permute-start(bf16[256,256]{1,0:T(8,128)(2,1)} %get-tuple-element.36), channel_id=1, source_target_pairs={{1,0},{2,1},{3,2},{4,3},{5,4},{6,5},{7,6},{8,7},{9,8},{10,9},{11,1... | collective-permute-start | bytes 393224 | tf_op jit(solution)/shard_map/ppermute | solution.py:741
  60.8 0.7 copy-start.3
  60.8 0.7 %copy-start.4 = (bf16[256,256]{1,0:T(8,128)(2,1)}, bf16[256,256]{1,0:T(8,128)(2,1)S(1)}, u32[]{:S(2)}) copy-start(bf16[256,256]{1,0:T(8,128)(2,1)S(1)} %collective-permute-done.3.refs_2_) | copy-start | bytes 393220
